TPU v7x, 32 devices: a whole 2x2x4 slice. The times are simulated.
32 devices in a mesh: freq: 32 (over z, y, x, core).
Axes of the slice: x: 2, y: 2, z: 4, core: 2. Of those that a mesh axis runs over, the one named last changes fastest.
Arguments:
- model_vis: bfloat16 [64, 8, 4096], P('freq'), may hold values from -6 to 6
- observed: float32 [64, 4096], P('freq'), may hold values from -48 to 48
- row_keep: int32 [64, 4096], P('freq'), may hold values 0 or 1
- station_one: int32 [4096], replicated, may hold values from 0 to 61, as said below
- station_two: int32 [4096], replicated, may hold values from 0 to 61
- smoothness: float32 [496], replicated, may hold values from 4 to 24576
Outputs:
- gains: float32 [64, 496], P('freq')
Inputs may be any that keep to these rules, and one draw needn't show every extreme that they name: station_one and station_two differ in every row.
All inputs are finite; a program needn't handle non-finite values. No bound on the sum of `row_keep` on one device may be relied on, other than what follows from the above.
Results may differ from a plain program's by a relative error of at most 0.0003.
Values sent between devices are 32-bit elements; how exact they have to be, the bound alone decides.
A program may use at most 256 MiB of HBM per device.

v0:
```python
import jax
import jax.numpy as jnp
from jax import lax
from jax.experimental import pallas as pl
from jax.experimental.pallas import tpu as pltpu
from jax.sharding import PartitionSpec as P

ridge_weight = 1.0
PANEL = 128
GROUP = 16
SUB = 8
PIVOTS = 4
HIGHEST = lax.Precision.HIGHEST


def mm(left, right, dims=((1,), (0,))):
    return lax.dot_general(
        left, right, (dims, ((), ())), precision=HIGHEST, preferred_element_type=jnp.float32
    )


NT = ((1,), (1,))
TN = ((0,), (0,))


def small_inverse(entries):
    size = len(entries)
    for m in range(size):
        inv = 1.0 / entries[m][m]
        scaled = [inv if j == m else entries[m][j] * inv for j in range(size)]
        entries = [
            scaled
            if i == m
            else [
                -(entries[i][m] * inv) if j == m else entries[i][j] - entries[i][m] * scaled[j]
                for j in range(size)
            ]
            for i in range(size)
        ]
    return entries


def invert_panel(block):
    size = block.shape[0]
    strips = size // SUB
    lane = lax.broadcasted_iota(jnp.int32, (SUB, size), 1)
    sub = lax.broadcasted_iota(jnp.int32, (SUB, size), 0)

    def spread(value):
        return jnp.broadcast_to(value, (SUB, size))

    def group(_, a):
        a = list(a)
        for k in range(0, GROUP, PIVOTS):
            home, offset = k // SUB, k % SUB
            rows = [spread(a[home][offset + i : offset + i + 1, :]) for i in range(PIVOTS)]
            entries = [
                [spread(row[:, k + j : k + j + 1]) for j in range(PIVOTS)] for row in rows
            ]
            inverse = small_inverse(entries)
            inside = (lane >= k) & (lane < k + PIVOTS)
            marked = [
                jnp.where(inside, jnp.where(lane == k + i, 1.0, 0.0), rows[i])
                for i in range(PIVOTS)
            ]
            scaled = [
                sum(inverse[i][j] * marked[j] for j in range(PIVOTS)) for i in range(PIVOTS)
            ]
            for t in range(strips):
                value = jnp.where(inside, 0.0, a[t])
                for i in range(PIVOTS):
                    value = value - spread(a[t][:, k + i : k + i + 1]) * scaled[i]
                if t == home:
                    for i in range(PIVOTS):
                        value = jnp.where(sub == offset + i, scaled[i], value)
                a[t] = value
        shift = GROUP // SUB
        return tuple(pltpu.roll(a[(t + shift) % strips], size - GROUP, 1) for t in range(strips))

    start = tuple(block[t * SUB : (t + 1) * SUB, :] for t in range(strips))
    return jnp.concatenate(lax.fori_loop(0, size // GROUP, group, start), axis=0)


def invert_in_place(a_ref, row_ref):
    width = a_ref.shape[0]

    @pl.loop(0, width // PANEL)
    def _(step):
        own = pl.ds(pl.multiple_of(step * PANEL, PANEL), PANEL)
        pivot = invert_panel(a_ref[own, own])
        row_ref[...] = mm(pivot, a_ref[own, :])
        row_ref[:, own] = pivot
        col = a_ref[:, own]
        a_ref[:, own] = jnp.zeros_like(col)
        a_ref[...] = a_ref[...] - mm(col, row_ref[...])
        a_ref[own, :] = row_ref[...]


def normal_kernel(vis_ref, obs_ref, keep_ref, one_ref, two_ref, normal_ref, target_ref):
    padded = normal_ref.shape[1]
    directions, rows = vis_ref.shape[1], vis_ref.shape[2]
    stations = padded // directions

    @pl.when(pl.program_id(1) == 0)
    def _():
        normal_ref[...] = jnp.zeros_like(normal_ref)
        target_ref[...] = jnp.zeros_like(target_ref)

    station = lax.broadcasted_iota(jnp.int32, (stations, rows), 0)
    touched = (station == one_ref[...]) | (station == two_ref[...])
    keep = keep_ref[0].astype(jnp.float32)
    vis = vis_ref[0].astype(jnp.float32)
    kept = touched & (keep > 0.0)
    plain = jnp.concatenate(
        [jnp.where(touched, vis[d : d + 1, :], 0.0) for d in range(directions)], axis=0
    ).astype(jnp.bfloat16)
    weighted = jnp.concatenate(
        [jnp.where(kept, vis[d : d + 1, :], 0.0) for d in range(directions)], axis=0
    ).astype(jnp.bfloat16)
    normal_ref[0] += lax.dot_general(
        weighted, plain, (NT, ((), ())), preferred_element_type=jnp.float32
    )
    data = obs_ref[0]
    high = data.astype(jnp.bfloat16).astype(jnp.float32)
    middle = (data - high).astype(jnp.bfloat16).astype(jnp.float32)
    low = data - high - middle
    pieces = jnp.concatenate([high, middle, low, jnp.zeros((5, rows), jnp.float32)], axis=0)
    target_ref[0] += lax.dot_general(
        pieces.astype(jnp.bfloat16), weighted, (NT, ((), ())), preferred_element_type=jnp.float32
    )


def first_kernel(diag_ref, source_ref, down_ref, across_ref, coupling_ref, y_ref, a_ref, row_ref):
    a_ref[...] = diag_ref[...]
    invert_in_place(a_ref, row_ref)
    y_ref[...] = mm(source_ref[...], a_ref[...])
    scaled = a_ref[...] * across_ref[...]
    coupling_ref[...] = scaled * down_ref[...]


def level_kernel(
    diag_ref, lower_ref, above_ref, source_ref,
    xr_ref, xl_ref, up_ref, down_ref, c_ref, y_ref, by_up_ref, by_down_ref, a_ref, row_ref,
):
    a_ref[...] = diag_ref[...]
    invert_in_place(a_ref, row_ref)
    xr_ref[...] = mm(above_ref[...], a_ref[...])
    xl_ref[...] = mm(lower_ref[...], a_ref[...], TN)
    up_ref[...] = mm(xr_ref[...], above_ref[...], NT)
    c_ref[...] = mm(xr_ref[...], lower_ref[...])
    down_ref[...] = mm(xl_ref[...], lower_ref[...])
    y = mm(source_ref[...], a_ref[...])
    y_ref[...] = y
    by_up_ref[...] = mm(y, above_ref[...], NT)
    by_down_ref[...] = mm(y, lower_ref[...])


def last_kernel(diag_ref, source_ref, y_ref, a_ref, row_ref):
    a_ref[...] = diag_ref[...]
    invert_in_place(a_ref, row_ref)
    y_ref[...] = mm(source_ref[...], a_ref[...])


def call(kernel, width, outs, *operands):
    vmem = pl.BlockSpec(memory_space=pltpu.VMEM)
    return pl.pallas_call(
        kernel,
        out_shape=[jax.ShapeDtypeStruct(o, jnp.float32) for o in outs],
        in_specs=[vmem] * len(operands),
        out_specs=[vmem] * len(outs),
        scratch_shapes=[
            pltpu.VMEM((width, width), jnp.float32),
            pltpu.VMEM((PANEL, width), jnp.float32),
        ],
        compiler_params=pltpu.CompilerParams(vmem_limit_bytes=48 << 20),
    )(*operands)


def normals(model_vis, observed, row_keep, station_one, station_two, padded):
    channels, directions, rows = model_vis.shape
    chunk = 1024 if rows % 1024 == 0 else rows
    return pl.pallas_call(
        normal_kernel,
        grid=(channels, rows // chunk),
        out_shape=[
            jax.ShapeDtypeStruct((channels, padded, padded), jnp.float32),
            jax.ShapeDtypeStruct((channels, 8, padded), jnp.float32),
        ],
        in_specs=[
            pl.BlockSpec((1, directions, chunk), lambda f, r: (f, 0, r)),
            pl.BlockSpec((1, 1, chunk), lambda f, r: (f, 0, r)),
            pl.BlockSpec((1, 1, chunk), lambda f, r: (f, 0, r)),
            pl.BlockSpec((1, chunk), lambda f, r: (0, r)),
            pl.BlockSpec((1, chunk), lambda f, r: (0, r)),
        ],
        out_specs=[
            pl.BlockSpec((1, padded, padded), lambda f, r: (f, 0, 0)),
            pl.BlockSpec((1, 8, padded), lambda f, r: (f, 0, 0)),
        ],
        compiler_params=pltpu.CompilerParams(vmem_limit_bytes=48 << 20),
    )(
        model_vis,
        observed.reshape(channels, 1, rows),
        row_keep.reshape(channels, 1, rows),
        station_one.reshape(1, rows),
        station_two.reshape(1, rows),
    )


def move(block, route):
    return lax.ppermute(block, "freq", route)


def body(model_vis, observed, row_keep, station_one, station_two, smoothness):
    channels, directions, _ = model_vis.shape
    assert channels == 2
    devices = lax.axis_size("freq")
    assert devices & (devices - 1) == 0
    position = lax.axis_index("freq")
    stations = smoothness.shape[0] // directions
    slots = -(-stations // 64) * 64
    width = directions * slots
    square, line = (width, width), (8, width)
    smooth = jnp.pad(
        smoothness.reshape(directions, stations), ((0, 0), (0, slots - stations))
    ).reshape(width)

    normal, pieces = normals(model_vis, observed, row_keep, station_one, station_two, width)
    targets = jnp.sum(pieces, axis=1)
    identity = jnp.eye(width, dtype=jnp.float32)

    def diagonal(local):
        channel = position * channels + local
        neighbours = (
            2.0
            - (channel == 0).astype(jnp.float32)
            - (channel == channels * devices - 1).astype(jnp.float32)
        )
        return normal[local] + identity * (ridge_weight + neighbours * smooth)[:, None]

    def as_line(vector):
        return jnp.pad(vector[None, :], ((0, 7), (0, 0)))

    coupling, y0 = call(
        first_kernel, width, (square, line),
        diagonal(0), as_line(targets[0]), smooth[:, None], smooth[None, :],
    )
    back = [(i, i - 1) for i in range(1, devices)]
    from_next = move(coupling, back)
    pulled = y0 * smooth[None, :]
    pulled_next = move(pulled, back)
    diag = diagonal(1) - coupling - from_next
    lower = -jnp.where(position > 0, coupling, 0.0)
    above = -from_next
    source = as_line(targets[1]) + pulled + pulled_next

    levels = (devices - 1).bit_length()
    kept = []
    for level in range(levels):
        stride = 1 << level
        xr, xl, up, down, cross, y, by_up, by_down = call(
            level_kernel, width, (square,) * 5 + (line,) * 3, diag, lower, above, source
        )
        kept.append((xr, xl, y))
        gone = range(stride - 1, devices, 2 * stride)
        rise = [(i, i + stride) for i in gone]
        fall = [(i, i - stride) for i in gone if i >= stride]
        next_gone = range(2 * stride - 1, devices, 4 * stride) if level + 1 < levels else ()
        if fall:
            diag = diag - move(up, rise) - move(down, fall)
            source = source - move(by_up, rise) - move(by_down, fall)
        else:
            diag = diag - move(up, rise)
            source = source - move(by_up, rise)
        if level + 1 < levels:
            lower = -move(cross, [(i, j) for i, j in rise if j in next_gone])
            above = -move(cross, [(i, j) for i, j in fall if j in next_gone])
    (gains,) = call(last_kernel, width, (line,), diag, source)
    for level in reversed(range(levels)):
        stride = 1 << level
        xr, xl, y = kept[level]
        gone = range(stride - 1, devices, 2 * stride)
        from_above = move(gains, [(i + stride, i) for i in gone])
        value = y - mm(from_above, xr)
        falling = [(i - stride, i) for i in gone if i >= stride]
        if falling:
            value = value - mm(move(gains, falling), xl)
        mine = lax.rem(position + 1, 2 * stride) == stride
        gains = jnp.where(mine, value, gains)
    earlier = move(gains, [(i, i + 1) for i in range(devices - 1)])
    scale = jnp.where(smooth > 0, 1.0 / jnp.where(smooth > 0, smooth, 1.0), 0.0)
    first = y0 + mm(earlier + gains, coupling) * scale[None, :]
    both = jnp.stack([first[0], gains[0]])
    return both.reshape(channels, directions, slots)[:, :, :stations].reshape(
        channels, directions * stations
    )


def solution(mesh):
    placed = (P("freq", None, None), P("freq", None), P("freq", None), P(), P(), P())
    return jax.shard_map(
        body, mesh=mesh, in_specs=placed, out_specs=P("freq", None), check_vma=False
    )
```

profile of v0, /device:TPU:8, one launch (start us, length us, event | category | flops | bytes accessed | tf_op | source)
XLA Modules:
  0.0 546.8 jit_solution(2095449091813657085)
XLA Ops:
  5.0 7.8 %shard_map.64 = (f32[2,512,512]{2,1,0:T(8,128)S(1)}, f32[2,8,512]{2,1,0:T(8,128)S(1)}) custom-call(bf16[2,8,4096]{2,1,0:T(8,128)(2,1)S(1)} %copy-done.7, f32[2,1,4096]{2,1,0:T(1,128)S(1)} %reshape.50.obs_ref, s32[2,1,4096]{2,1,0:T(1,128)S(1)} %reshape.51.keep_ref, s32[1,4096]{1,0:T(1,128)S(1)} %bitcast.30, s32[1,4096]{1,0:T(1,128)S(1)} %bitcast.31), custom_call_target="tpu_custom_call" | custom-call | tf_op jit(solution)/shard_map/pallas_call | solution.py:182
  13.1 31.9 %shard_map.65 = (f32[512,512]{1,0:T(8,128)S(1)}, f32[8,512]{1,0:T(8,128)S(1)}) custom-call(f32[512,512]{1,0:T(8,128)S(1)} %bitcast_add_fusion.1.diag_ref, f32[8,512]{1,0:T(8,128)S(1)} %pad.12.source_ref, f32[512,1]{1,0:T(8,128)S(1)} %reshape.59.down_ref, f32[1,512]{1,0:T(1,128)S(1)} %broadcast_in_dim_reshape.2.across_ref), custom_call_target="tpu_custom_call" | custom-call | tf_op jit(solution)/shard_map/pallas_call | solution.py:166
  45.0 7.2 %collective-permute-start = (f32[512,512]{1,0:T(8,128)S(1)}, f32[512,512]{1,0:T(8,128)}, u32[]{:S(2)}, u32[]{:S(2)}) collective-permute-start(f32[512,512]{1,0:T(8,128)S(1)} %get-tuple-element.48), channel_id=1, source_target_pairs={{1,0},{2,1},{3,2},{4,3},{5,4},{6,5},{7,6},{8,7},{9,8},{10,9},{11,1... | collective-permute-start | bytes 3145736 | tf_op jit(solution)/shard_map/ppermute | solution.py:211
  52.3 7.7 %collective-permute-start.1 = (f32[8,512]{1,0:T(8,128)S(1)}, f32[8,512]{1,0:T(8,128)S(1)}, u32[]{:S(2)}, u32[]{:S(2)}) collective-permute-start(f32[8,512]{1,0:T(8,128)S(1)} %broadcast_multiply_fusion), channel_id=1, source_target_pairs={{1,0},{2,1},{3,2},{4,3},{5,4},{6,5},{7,6},{8,7},{9,8},{10,9},{11,1... | collective-permute-start | bytes 49160 | tf_op jit(solution)/shard_map/ppermute | solution.py:211
  60.0 4.7 collective-permute-done.1
  64.8 3.3 fusion.4
  68.1 43.5 %shard_map.66 = (f32[512,512]{1,0:T(8,128)S(1)}, f32[512,512]{1,0:T(8,128)S(1)}, f32[512,512]{1,0:T(8,128)S(1)}, f32[512,512]{1,0:T(8,128)S(1)}, f32[512,512]{1,...) custom-call(f32[512,512]{1,0:T(8,128)} %get-tuple-element.86.diag_ref, ...), custom_call_target="tpu_custom_call" | custom-call | tf_op jit(solution)/shard_map/pallas_call | solution.py:166
  111.5 3.7 collective-permute-start.4
  116.0 2.3 collective-permute-start.2
  118.2 2.1 collective-permute-start.3
  122.5 3.7 collective-permute-start.7
  126.2 6.6 %collective-permute-done.7 = f32[8,512]{1,0:T(8,128)S(1)} collective-permute-done((f32[8,512]{1,0:T(8,128)S(1)}, f32[8,512]{1,0:T(8,128)S(1)}, u32[]{:S(2)}, u32[]{:S(2)}) %collective-permute-start.7) | collective-permute-done | bytes 16416 | tf_op jit(solution)/shard_map/ppermute | solution.py:211
  136.3 43.3 %shard_map.67 = (f32[512,512]{1,0:T(8,128)S(1)}, f32[512,512]{1,0:T(8,128)S(1)}, f32[512,512]{1,0:T(8,128)S(1)}, f32[512,512]{1,0:T(8,128)S(1)}, f32[512,512]{1,...) custom-call(f32[512,512]{1,0:T(8,128)} %subtract_subtract_fusion.3.diag_ref, ...), custom_call_target="tpu_custom_call" | custom-call | tf_op jit(solution)/shard_map/pallas_call | solution.py:166
  187.7 43.3 %shard_map.68 = (f32[512,512]{1,0:T(8,128)S(1)}, f32[512,512]{1,0:T(8,128)S(1)}, f32[512,512]{1,0:T(8,128)S(1)}, f32[512,512]{1,0:T(8,128)S(1)}, f32[512,512]{1,...) custom-call(f32[512,512]{1,0:T(8,128)} %subtract_subtract_fusion.2.diag_ref, ...), custom_call_target="tpu_custom_call" | custom-call | tf_op jit(solution)/shard_map/pallas_call | solution.py:166
  239.3 43.3 %shard_map.69 = (f32[512,512]{1,0:T(8,128)S(1)}, f32[512,512]{1,0:T(8,128)S(1)}, f32[512,512]{1,0:T(8,128)S(1)}, f32[512,512]{1,0:T(8,128)S(1)}, f32[512,512]{1,...) custom-call(f32[512,512]{1,0:T(8,128)} %subtract_subtract_fusion.1.diag_ref, ...), custom_call_target="tpu_custom_call" | custom-call | tf_op jit(solution)/shard_map/pallas_call | solution.py:166
  290.7 44.4 %shard_map.70 = (f32[512,512]{1,0:T(8,128)S(1)}, f32[512,512]{1,0:T(8,128)}, f32[512,512]{1,0:T(8,128)S(1)}, f32[512,512]{1,0:T(8,128)}, f32[512,512]{1,0:T(8,12...) custom-call(f32[512,512]{1,0:T(8,128)} %subtract_subtract_fusion.diag_ref, ...), custom_call_target="tpu_custom_call" | custom-call | tf_op jit(solution)/shard_map/pallas_call | solution.py:166
  337.9 31.9 %shard_map.71 = f32[8,512]{1,0:T(8,128)S(1)} custom-call(f32[512,512]{1,0:T(8,128)S(1)} %sub.121.diag_ref, f32[8,512]{1,0:T(8,128)S(1)} %sub.122.source_ref), custom_call_target="tpu_custom_call" | custom-call | tf_op jit(solution)/shard_map/pallas_call | solution.py:166
  375.5 1.8 subtract_select_fusion.3
  380.5 1.8 subtract_select_fusion.2
  385.6 1.8 subtract_select_fusion.1
  390.0 145.2 %collective-permute-done.35 = f32[8,512]{1,0:T(8,128)S(1)} collective-permute-done((f32[8,512]{1,0:T(8,128)S(1)}, f32[8,512]{1,0:T(8,128)S(1)}, u32[]{:S(2)}, u32[]{:S(2)}) %collective-permute-start.35) | collective-permute-done | bytes 16416 | tf_op jit(solution)/shard_map/ppermute | solution.py:211
  535.8 2.0 collective-permute-done.36
  538.4 1.9 collective-permute-start.37
  540.3 4.9 collective-permute-done.37
  (139 shorter events, 55.8 us)
Async XLA Ops:
  45.0 19.7 %collective-permute-start = (f32[512,512]{1,0:T(8,128)S(1)}, f32[512,512]{1,0:T(8,128)}, u32[]{:S(2)}, u32[]{:S(2)}) collective-permute-start(f32[512,512]{1,0:T(8,128)S(1)} %get-tuple-element.48), channel_id=1, source_target_pairs={{1,0},{2,1},{3,2},{4,3},{5,4},{6,5},{7,6},{8,7},{9,8},{10,9},{11,1... | collective-permute-start | bytes 3145736 | tf_op jit(solution)/shard_map/ppermute | solution.py:211
  52.3 12.5 %collective-permute-start.1 = (f32[8,512]{1,0:T(8,128)S(1)}, f32[8,512]{1,0:T(8,128)S(1)}, u32[]{:S(2)}, u32[]{:S(2)}) collective-permute-start(f32[8,512]{1,0:T(8,128)S(1)} %broadcast_multiply_fusion), channel_id=1, source_target_pairs={{1,0},{2,1},{3,2},{4,3},{5,4},{6,5},{7,6},{8,7},{9,8},{10,9},{11,1... | collective-permute-start | bytes 49160 | tf_op jit(solution)/shard_map/ppermute | solution.py:211
  111.5 21.3 %collective-permute-start.4 = (f32[512,512]{1,0:T(8,128)S(1)}, f32[512,512]{1,0:T(8,128)S(1)}, u32[]{:S(2)}, u32[]{:S(2)}) collective-permute-start(f32[512,512]{1,0:T(8,128)S(1)} %get-tuple-element.52), channel_id=1, source_target_pairs={{0,1},{4,5},{8,9},{12,13},{16,17},{20,21},{24,25},{28,29}} | collective-permute-start | bytes 3145736 | tf_op jit(solution)/shard_map/ppermute | solution.py:211
  115.2 18.6 %collective-permute-start.5 = (f32[512,512]{1,0:T(8,128)S(1)}, f32[512,512]{1,0:T(8,128)S(1)}, u32[]{:S(2)}, u32[]{:S(2)}) collective-permute-start(f32[512,512]{1,0:T(8,128)S(1)} %get-tuple-element.52), channel_id=1, source_target_pairs={{2,1},{6,5},{10,9},{14,13},{18,17},{22,21},{26,25},{30,29}} | collective-permute-start | bytes 3145736 | tf_op jit(solution)/shard_map/ppermute | solution.py:211
  116.0 19.0 %collective-permute-start.2 = (f32[512,512]{1,0:T(8,128)S(1)}, f32[512,512]{1,0:T(8,128)S(1)}, u32[]{:S(2)}, u32[]{:S(2)}) collective-permute-start(f32[512,512]{1,0:T(8,128)S(1)} %get-tuple-element.50), channel_id=1, source_target_pairs={{0,1},{2,3},{4,5},{6,7},{8,9},{10,11},{12,13},{14,15},{16,17},{18,... | collective-permute-start | bytes 3145736 | tf_op jit(solution)/shard_map/ppermute | solution.py:211
  118.2 16.7 %collective-permute-start.3 = (f32[512,512]{1,0:T(8,128)S(1)}, f32[512,512]{1,0:T(8,128)S(1)}, u32[]{:S(2)}, u32[]{:S(2)}) collective-permute-start(f32[512,512]{1,0:T(8,128)S(1)} %get-tuple-element.51), channel_id=1, source_target_pairs={{2,1},{4,3},{6,5},{8,7},{10,9},{12,11},{14,13},{16,15},{18,17},{20... | collective-permute-start | bytes 3145736 | tf_op jit(solution)/shard_map/ppermute | solution.py:211
  122.5 10.3 %collective-permute-start.7 = (f32[8,512]{1,0:T(8,128)S(1)}, f32[8,512]{1,0:T(8,128)S(1)}, u32[]{:S(2)}, u32[]{:S(2)}) collective-permute-start(f32[8,512]{1,0:T(8,128)S(1)} %get-tuple-element.54), channel_id=1, source_target_pairs={{2,1},{4,3},{6,5},{8,7},{10,9},{12,11},{14,13},{16,15},{18,17},{20... | collective-permute-start | bytes 49160 | tf_op jit(solution)/shard_map/ppermute | solution.py:211
  179.6 4.5 collective-permute-start.10
  180.3 4.9 collective-permute-start.11
  181.0 5.2 collective-permute-start.8
  182.0 4.3 collective-permute-start.9
  230.9 4.7 collective-permute-start.16
  231.7 5.1 collective-permute-start.17
  232.4 5.5 %collective-permute-start.14 = (f32[512,512]{1,0:T(8,128)S(1)}, f32[512,512]{1,0:T(8,128)S(1)}, u32[]{:S(2)}, u32[]{:S(2)}) collective-permute-start(f32[512,512]{1,0:T(8,128)S(1)} %get-tuple-element.62), channel_id=1, source_target_pairs={{3,7},{11,15},{19,23},{27,31}} | collective-permute-start | bytes 3145736 | tf_op jit(solution)/shard_map/ppermute | solution.py:211
  233.6 4.4 collective-permute-start.15
  282.6 4.5 collective-permute-start.22
  283.3 4.9 collective-permute-start.23
  284.0 5.3 collective-permute-start.20
  285.0 4.4 collective-permute-start.21
  373.0 2.5 collective-permute-start.30
  378.0 2.5 collective-permute-start.32
  387.4 147.8 %collective-permute-start.35 = (f32[8,512]{1,0:T(8,128)S(1)}, f32[8,512]{1,0:T(8,128)S(1)}, u32[]{:S(2)}, u32[]{:S(2)}) collective-permute-start(f32[8,512]{1,0:T(8,128)S(1)} %subtract_select_fusion.1), channel_id=1, source_target_pairs={{1,0},{3,2},{5,4},{7,6},{9,8},{11,10},{13,12},{15,14},{17,16},{19,... | collective-permute-start | bytes 49160 | tf_op jit(solution)/shard_map/ppermute | solution.py:211
  388.7 149.1 %collective-permute-start.36 = (f32[8,512]{1,0:T(8,128)S(1)}, f32[8,512]{1,0:T(8,128)S(1)}, u32[]{:S(2)}, u32[]{:S(2)}) collective-permute-start(f32[8,512]{1,0:T(8,128)S(1)} %subtract_select_fusion.1), channel_id=1, source_target_pairs={{1,2},{3,4},{5,6},{7,8},{9,10},{11,12},{13,14},{15,16},{17,18},{19... | collective-permute-start | bytes 49160 | tf_op jit(solution)/shard_map/ppermute | solution.py:211
  538.4 6.9 %collective-permute-start.37 = (f32[8,512]{1,0:T(8,128)S(1)}, f32[8,512]{1,0:T(8,128)S(1)}, u32[]{:S(2)}, u32[]{:S(2)}) collective-permute-start(f32[8,512]{1,0:T(8,128)S(1)} %subtract_select_fusion), channel_id=1, source_target_pairs={{0,1},{1,2},{2,3},{3,4},{4,5},{5,6},{6,7},{7,8},{8,9},{9,10},{10,1... | collective-permute-start | bytes 49160 | tf_op jit(solution)/shard_map/ppermute | solution.py:211
  (29 other events, 116.1 us)
where the time goes:
time: 552 us; the launch traced here: 547 us
  Pallas kernels  289 us (52%)
  waiting for transfers between devices  164 us (30%)
  starting transfers between devices  52.9 us (10%)
  other arithmetic  17.9 us (3%)
  matrix products  14.7 us (3%)
  local copies, waits for them, and re-layouts  6.88 us (1%)
    pallas_call x7, Pallas kernels, call(): pl.pallas_call(kernel, out_shape=[jax.ShapeDtypeStruct(o, jnp.float32) fo...  281 us
    ppermute x38, waiting for transfers between devices, move(): return lax.ppermute(block, 'freq', route)  164 us
    ppermute x38, starting transfers between devices, move(): return lax.ppermute(block, 'freq', route)  52.9 us
    dot_general x10, matrix products, mm(): lax.dot_general(left, right, (dims, ((), ())), precision=HIGHEST, preferr...  14.7 us
  transfers between devices with their start and end apart: 38, of which 6 were waited for; matrix products, arithmetic and copies ran while one was open for 3% of the time, Pallas kernels for 0%

commit v1 on v0

v1 whole, which is shorter than its diff:
```python
import functools

import jax
import jax.numpy as jnp
from jax import lax
from jax.experimental import pallas as pl
from jax.experimental.pallas import tpu as pltpu
from jax.sharding import PartitionSpec as P

ridge_weight = 1.0
PANEL = 128
SUB = 8
PIVOTS = 4
BLK = 32
HIGHEST = lax.Precision.HIGHEST


def mm(left, right, dims=((1,), (0,))):
    return lax.dot_general(
        left, right, (dims, ((), ())), precision=HIGHEST, preferred_element_type=jnp.float32
    )


NT = ((1,), (1,))
TN = ((0,), (0,))


def factor_panel(block):
    size = block.shape[0]
    strips = size // SUB
    lane = lax.broadcasted_iota(jnp.int32, (SUB, size), 1)
    sub = lax.broadcasted_iota(jnp.int32, (SUB, size), 0)
    index = range(PIVOTS)

    def spread(value):
        return jnp.broadcast_to(value, (SUB, size))

    def columns(value, k):
        return [jnp.take_along_axis(value, jnp.full((SUB, size), k + j, jnp.int32), axis=1) for j in index]

    a = [block[t * SUB : (t + 1) * SUB, :] for t in range(strips)]
    done = [jnp.zeros((SUB, size), jnp.float32) for _ in range(strips)]

    for k in range(0, size, PIVOTS):
        home, offset = k // SUB, k % SUB
        last = (k // BLK + 1) * BLK // SUB
        cols = columns(a[home], k)
        e = [[spread(cols[j][offset + i : offset + i + 1, :]) for j in range(i + 1)] for i in index]
        inverse, low = [], [[None] * PIVOTS for _ in index]
        for m in index:
            inverse.append(1.0 / e[m][m])
            for i in range(m + 1, PIVOTS):
                low[i][m] = e[i][m] * inverse[m]
                for j in range(m + 1, i + 1):
                    e[i][j] = e[i][j] - low[i][m] * e[j][m]
        inside = (lane >= k) & (lane < k + PIVOTS)
        u = []
        for i in index:
            row = spread(a[home][offset + i : offset + i + 1, :])
            value = jnp.where(inside, jnp.where(lane == k + i, 1.0, 0.0), row)
            for m in range(i):
                value = value - low[i][m] * u[m]
            u.append(value)
        s = [u[i] * inverse[i] for i in index]
        for i in reversed(index):
            for m in range(i + 1, PIVOTS):
                s[i] = s[i] - low[m][i] * s[m]
        for t in range((k + PIVOTS) // SUB, last):
            c = cols if t == home else columns(a[t], k)
            value = jnp.where(inside, 0.0, a[t])
            for j in index:
                value = value - c[j] * s[j]
            a[t] = value
        for i in index:
            root = lax.rsqrt(e[i][i])
            root = root * (1.5 - 0.5 * e[i][i] * root * root)
            done[home] = jnp.where(sub == offset + i, root * u[i], done[home])
        if offset + PIVOTS == SUB:
            keep = (lane <= sub + home * SUB) | (lane >= last * SUB)
            done[home] = jnp.where(keep, done[home], 0.0)
        if k + PIVOTS == last * SUB and last < strips:
            first = last - BLK // SUB
            rows = jnp.concatenate(done[first:last], axis=0)
            own = (lane >= first * SUB) & (lane < last * SUB)
            rest = jnp.concatenate([jnp.where(own, 0.0, a[t]) for t in range(last, strips)], axis=0)
            f = jnp.transpose(rows[:, last * SUB:])
            rest = rest - mm(f, rows)
            for t in range(last, strips):
                a[t] = rest[(t - last) * SUB : (t - last + 1) * SUB, :]
            for t in range(first, last):
                done[t] = jnp.where(lane < last * SUB, done[t], 0.0)
    return jnp.concatenate(done, axis=0)

def pairs(width):
    count = width // PANEL
    return [(r, c, r * (r + 1) // 2 + c) for r in range(count) for c in range(r + 1)]


def cut(index):
    return slice(index * PANEL, (index + 1) * PANEL)


def payload_rows(width):
    return len(pairs(width)) * PANEL + width // PANEL * SUB


def put_line(packed_ref, value):
    width = value.shape[1]
    base = len(pairs(width)) * PANEL
    for b in range(width // PANEL):
        packed_ref[base + b * SUB : base + (b + 1) * SUB, :] = value[:, cut(b)]


def get_line(packed_ref, width):
    base = len(pairs(width)) * PANEL
    return jnp.concatenate(
        [packed_ref[base + b * SUB : base + (b + 1) * SUB, :] for b in range(width // PANEL)], axis=1
    )


def fill_square(square_ref, packed_ref):
    for r, c, at in pairs(square_ref.shape[0]):
        piece = packed_ref[cut(at), :]
        square_ref[cut(r), cut(c)] = piece
        if r != c:
            square_ref[cut(c), cut(r)] = jnp.transpose(piece)


def factor(x_ref):
    width = x_ref.shape[0]
    count = width // PANEL

    @pl.loop(0, count)
    def _(step):
        own = pl.ds(pl.multiple_of(step * PANEL, PANEL), PANEL)
        x_ref[own, own] = factor_panel(x_ref[own, own])
        for p in range(count):

            @pl.when(step == p)
            def _():
                lo, hi = p * PANEL, (p + 1) * PANEL
                root = x_ref[lo:hi, lo:hi]
                if p:
                    x_ref[lo:hi, :lo] = mm(root, x_ref[lo:hi, :lo])
                if hi < width:
                    f = mm(x_ref[hi:, lo:hi], root, NT)
                    x_ref[hi:, hi:] = x_ref[hi:, hi:] - mm(f, f, NT)
                    if p:
                        x_ref[hi:, :lo] = x_ref[hi:, :lo] - mm(f, x_ref[lo:hi, :lo])
                    x_ref[hi:, lo:hi] = -mm(f, root)

    for r in range(count - 1):
        x_ref[cut(r), (r + 1) * PANEL :] = jnp.zeros((PANEL, width - (r + 1) * PANEL), jnp.float32)


def first_kernel(diag_ref, source_ref, across_ref, coupling_ref, packed_ref, y_ref, x_ref, t_ref):
    width = diag_ref.shape[0]
    x_ref[...] = diag_ref[...]
    factor(x_ref)
    y = mm(mm(source_ref[...], x_ref[...], NT), x_ref[...])
    y_ref[...] = y
    put_line(packed_ref, y * across_ref[...])
    x_ref[...] = x_ref[...] * across_ref[...]
    for r, c, _ in pairs(width):
        t_ref[cut(c), cut(r)] = jnp.transpose(x_ref[cut(r), cut(c)])
    for r in range(width // PANEL):
        value = mm(t_ref[cut(r), r * PANEL :], x_ref[r * PANEL :, : (r + 1) * PANEL])
        for c in range(r + 1):
            packed_ref[cut(r * (r + 1) // 2 + c), :] = value[:, cut(c)]
    fill_square(coupling_ref, packed_ref)


def level_kernel(first, flag_ref, diag_ref, rise_ref, fall_ref, below_ref, *refs):
    if first:
        source_ref, *outs, above_ref = refs
    else:
        above_ref, source_ref, *outs = refs
    diag_out, source_out, up_ref, down_ref, cross_ref, c_ref, line_ref, x_ref = outs
    width = diag_ref.shape[0]
    for r, c, at in pairs(width):
        diag_out[cut(r), cut(c)] = (
            diag_ref[cut(r), cut(c)] - rise_ref[cut(at), :] - fall_ref[cut(at), :]
        )
    source_out[...] = source_ref[...] + get_line(rise_ref, width) + get_line(fall_ref, width)

    @pl.when(flag_ref[0] == 1)
    def _():
        if first:
            fill_square(above_ref, fall_ref)
        x_ref[...] = diag_out[...]
        factor(x_ref)
        half = width // 2
        for side, ref in enumerate((below_ref, above_ref)):
            c_ref[side, :, :half] = mm(ref[:, :half], x_ref[:half, :half], NT)
            c_ref[side, :, half:] = mm(ref[...], x_ref[half:, :], NT)
        line = mm(source_out[...], x_ref[...], NT)
        line_ref[...] = line
        cross_ref[...] = mm(c_ref[flag_ref[1]], c_ref[1 - flag_ref[1]], NT)
        for side, ref in enumerate((down_ref, up_ref)):
            put_line(ref, mm(line, c_ref[side], NT))
            for r in range(width // PANEL):
                value = mm(c_ref[side, cut(r), :], c_ref[side, : (r + 1) * PANEL, :], NT)
                for c in range(r + 1):
                    ref[cut(r * (r + 1) // 2 + c), :] = value[:, cut(c)]


def last_kernel(diag_ref, rise_ref, source_ref, y_ref, x_ref):
    width = diag_ref.shape[0]
    for r, c, at in pairs(width):
        x_ref[cut(r), cut(c)] = diag_ref[cut(r), cut(c)] - rise_ref[cut(at), :]
    factor(x_ref)
    source = source_ref[...] + get_line(rise_ref, width)
    y_ref[...] = mm(mm(source, x_ref[...], NT), x_ref[...])


def back_kernel(flag_ref, below_ref, above_ref, gains_ref, c_ref, line_ref, x_ref, out_ref):
    out_ref[...] = gains_ref[...]

    @pl.when(flag_ref[0] == 1)
    def _():
        line = line_ref[...] + mm(below_ref[...], c_ref[0]) + mm(above_ref[...], c_ref[1])
        out_ref[...] = mm(line, x_ref[...])


def call(kernel, outs, *operands, scratch=()):
    vmem = pl.BlockSpec(memory_space=pltpu.VMEM)
    smem = pl.BlockSpec(memory_space=pltpu.SMEM)
    return pl.pallas_call(
        kernel,
        out_shape=[jax.ShapeDtypeStruct(o, jnp.float32) for o in outs],
        in_specs=[smem if o.dtype == jnp.int32 else vmem for o in operands],
        out_specs=[vmem] * len(outs),
        scratch_shapes=[pltpu.VMEM(s, jnp.float32) for s in scratch],
        compiler_params=pltpu.CompilerParams(vmem_limit_bytes=48 << 20),
    )(*operands)

def normal_kernel(vis_ref, obs_ref, keep_ref, one_ref, two_ref, normal_ref, target_ref):
    padded = normal_ref.shape[1]
    directions, rows = vis_ref.shape[1], vis_ref.shape[2]
    stations = padded // directions

    @pl.when(pl.program_id(1) == 0)
    def _():
        normal_ref[...] = jnp.zeros_like(normal_ref)
        target_ref[...] = jnp.zeros_like(target_ref)

    station = lax.broadcasted_iota(jnp.int32, (stations, rows), 0)
    touched = (station == one_ref[...]) | (station == two_ref[...])
    keep = keep_ref[0].astype(jnp.float32)
    vis = vis_ref[0].astype(jnp.float32)
    kept = touched & (keep > 0.0)
    plain = jnp.concatenate(
        [jnp.where(touched, vis[d : d + 1, :], 0.0) for d in range(directions)], axis=0
    ).astype(jnp.bfloat16)
    weighted = jnp.concatenate(
        [jnp.where(kept, vis[d : d + 1, :], 0.0) for d in range(directions)], axis=0
    ).astype(jnp.bfloat16)
    normal_ref[0] += lax.dot_general(
        weighted, plain, (NT, ((), ())), preferred_element_type=jnp.float32
    )
    data = obs_ref[0]
    high = data.astype(jnp.bfloat16).astype(jnp.float32)
    middle = (data - high).astype(jnp.bfloat16).astype(jnp.float32)
    low = data - high - middle
    pieces = jnp.concatenate([high, middle, low, jnp.zeros((5, rows), jnp.float32)], axis=0)
    target_ref[0] += lax.dot_general(
        pieces.astype(jnp.bfloat16), weighted, (NT, ((), ())), preferred_element_type=jnp.float32
    )


def normals(model_vis, observed, row_keep, station_one, station_two, padded):
    channels, directions, rows = model_vis.shape
    chunk = 1024 if rows % 1024 == 0 else rows
    return pl.pallas_call(
        normal_kernel,
        grid=(channels, rows // chunk),
        out_shape=[
            jax.ShapeDtypeStruct((channels, padded, padded), jnp.float32),
            jax.ShapeDtypeStruct((channels, 8, padded), jnp.float32),
        ],
        in_specs=[
            pl.BlockSpec((1, directions, chunk), lambda f, r: (f, 0, r)),
            pl.BlockSpec((1, 1, chunk), lambda f, r: (f, 0, r)),
            pl.BlockSpec((1, 1, chunk), lambda f, r: (f, 0, r)),
            pl.BlockSpec((1, chunk), lambda f, r: (0, r)),
            pl.BlockSpec((1, chunk), lambda f, r: (0, r)),
        ],
        out_specs=[
            pl.BlockSpec((1, padded, padded), lambda f, r: (f, 0, 0)),
            pl.BlockSpec((1, 8, padded), lambda f, r: (f, 0, 0)),
        ],
        compiler_params=pltpu.CompilerParams(vmem_limit_bytes=48 << 20),
    )(
        model_vis,
        observed.reshape(channels, 1, rows),
        row_keep.reshape(channels, 1, rows),
        station_one.reshape(1, rows),
        station_two.reshape(1, rows),
    )


def move(block, route):
    return lax.ppermute(block, "freq", route)


def body(model_vis, observed, row_keep, station_one, station_two, smoothness):
    channels, directions, _ = model_vis.shape
    assert channels == 2
    devices = lax.axis_size("freq")
    assert devices & (devices - 1) == 0
    position = lax.axis_index("freq")
    stations = smoothness.shape[0] // directions
    slots = -(-stations // 64) * 64
    width = directions * slots
    square, line = (width, width), (SUB, width)
    packed = (payload_rows(width), PANEL)
    smooth = jnp.pad(
        smoothness.reshape(directions, stations), ((0, 0), (0, slots - stations))
    ).reshape(width)

    normal, pieces = normals(model_vis, observed, row_keep, station_one, station_two, width)
    targets = jnp.sum(pieces, axis=1)
    identity = jnp.eye(width, dtype=jnp.float32)

    def diagonal(local):
        channel = position * channels + local
        neighbours = (
            2.0
            - (channel == 0).astype(jnp.float32)
            - (channel == channels * devices - 1).astype(jnp.float32)
        )
        return normal[local] + identity * (ridge_weight + neighbours * smooth)[:, None]

    def as_line(vector):
        return jnp.pad(vector[None, :], ((0, SUB - 1), (0, 0)))

    coupling, rise, y0 = call(
        first_kernel, (square, packed, line),
        diagonal(0), as_line(targets[0]), smooth[None, :], scratch=(square, square),
    )
    fall = move(rise, [(i, i - 1) for i in range(1, devices)])
    diag, source, below, above = diagonal(1), as_line(targets[1]), coupling, None

    levels = (devices - 1).bit_length()
    kept = []
    for level in range(levels):
        stride = 1 << level
        phase = lax.rem(position + 1, 4 * stride)
        mine = lax.rem(phase, 2 * stride) == stride
        drop = (phase == 3 * stride).astype(jnp.int32)
        flag = jnp.stack([mine.astype(jnp.int32), drop])
        sides = (below,) if level == 0 else (below, above)
        diag, source, up, down, cross, c, solved, inverse = call(
            functools.partial(level_kernel, level == 0),
            (square, line, packed, packed, square, (2,) + square, line, square),
            flag, diag, rise, fall, *sides, source, scratch=(square,) * (level == 0),
        )
        kept.append((flag, c, solved, inverse))
        gone = range(stride - 1, devices, 2 * stride)
        rises = [(i, i + stride) for i in gone]
        falls = [(i, i - stride) for i in gone if i >= stride]
        next_gone = range(2 * stride - 1, devices, 4 * stride) if level + 1 < levels else ()
        if next_gone:
            below = move(cross, [(i, j) for i, j in rises if j in next_gone])
            above = move(cross, [(i, j) for i, j in falls if j in next_gone])
        rise = move(up, rises)
        if falls:
            fall = move(down, falls)
    (gains,) = call(last_kernel, (line,), diag, rise, source, scratch=(square,))
    for level in reversed(range(levels)):
        stride = 1 << level
        flag, c, solved, inverse = kept[level]
        gone = range(stride - 1, devices, 2 * stride)
        from_above = move(gains, [(i + stride, i) for i in gone])
        falling = [(i - stride, i) for i in gone if i >= stride]
        from_below = move(gains, falling) if falling else jnp.zeros_like(gains)
        (gains,) = call(back_kernel, (line,), flag, from_below, from_above, gains, c, solved, inverse)
    earlier = move(gains, [(i, i + 1) for i in range(devices - 1)])
    scale = jnp.where(smooth > 0, 1.0 / jnp.where(smooth > 0, smooth, 1.0), 0.0)
    first = y0 + mm(earlier + gains, coupling) * scale[None, :]
    both = jnp.stack([first[0], gains[0]])
    return both.reshape(channels, directions, slots)[:, :, :stations].reshape(
        channels, directions * stations
    )


def solution(mesh):
    placed = (P("freq", None, None), P("freq", None), P("freq", None), P(), P(), P())
    return jax.shard_map(
        body, mesh=mesh, in_specs=placed, out_specs=P("freq", None), check_vma=False
    )
```

time: 552 us -> 470 us (0.85)
  Pallas kernels: 289 us -> 146 us
  waiting for transfers between devices: 164 us -> 260 us
  other arithmetic: 17.9 us -> 1.72 us
  starting transfers between devices: 52.9 us -> 36.9 us
  matrix products: 14.7 us -> 0.61 us
  local copies, waits for them, and re-layouts: 6.88 us -> 18 us
    pallas_call x7 -> x12, Pallas kernels: 281 us -> 138 us  [call(): pl.pallas_call(kernel, out_shape=[jax.ShapeDtypeStruct(o, jnp.float32) fo...]
    ppermute x38 -> x28, waiting for transfers between devices: 164 us -> 260 us  [move(): return lax.ppermute(block, 'freq', route)]
    ppermute x38 -> x28, starting transfers between devices: 52.9 us -> 36.9 us  [move(): return lax.ppermute(block, 'freq', route)]
    dot_general x10 -> x1, matrix products: 14.7 us -> 0.61 us  [mm(): lax.dot_general(left, right, (dims, ((), ())), precision=HIGHEST, preferr...]
    neg x9 -> x0, other arithmetic: 12.1 us -> none  [the longest x4 4.39 us: body(): lower = -move(cross, [(i, j) for i, j in rise if j in next_gone])]
    unnamed x30 -> x42, local copies, waits for them, and re-layouts: 3.43 us -> 14.8 us
    sub x10 -> x0, other arithmetic: 5.59 us -> none  [the longest x4 5.34 us: body(): diag = diag - move(up, rise) - move(down, fall)]
  transfers between devices with their start and end apart: 38 -> 28, of which waited for: 6 -> 6; matrix products, arithmetic and copies ran while one was open for 3% -> 0% of each run, Pallas kernels for 0% -> 0%
where the time goes in v1:
time: 470 us; the launch traced here: 464 us
  waiting for transfers between devices  260 us (55%)
  Pallas kernels  146 us (31%)
  starting transfers between devices  36.9 us (8%)
  local copies, waits for them, and re-layouts  18 us (4%)
    ppermute x28, waiting for transfers between devices, move(): return lax.ppermute(block, 'freq', route)  260 us
    pallas_call x12, Pallas kernels, call(): pl.pallas_call(kernel, out_shape=[jax.ShapeDtypeStruct(o, jnp.float32) fo...  138 us
    ppermute x28, starting transfers between devices, move(): return lax.ppermute(block, 'freq', route)  36.9 us
    unnamed x42, local copies, waits for them, and re-layouts  14.8 us
  transfers between devices with their start and end apart: 28, of which 6 were waited for; matrix products, arithmetic and copies ran while one was open for 0% of the time, Pallas kernels for 0%

profile of v1, /device:TPU:8, one launch (start us, length us, event | category | flops | bytes accessed | tf_op | source)
XLA Modules:
  0.0 463.6 jit_solution(10229668755837538061)
XLA Ops:
  4.8 7.9 %shard_map.64 = (f32[2,512,512]{2,1,0:T(8,128)S(1)}, f32[2,8,512]{2,1,0:T(8,128)S(1)}) custom-call(bf16[2,8,4096]{2,1,0:T(8,128)(2,1)S(1)} %copy-done.17, f32[2,1,4096]{2,1,0:T(1,128)S(1)} %reshape.47.obs_ref, s32[2,1,4096]{2,1,0:T(1,128)S(1)} %reshape.48.keep_ref, s32[1,4096]{1,0:T(1,128)S(1)} %bitcast.18, s32[1,4096]{1,0:T(1,128)S(1)} %bitcast.19), custom_call_target="tpu_custom_call" | custom-call | tf_op jit(solution)/shard_map/pallas_call | solution.py:274
  14.1 27.1 %shard_map.65 = (f32[512,512]{1,0:T(8,128)S(1)}, f32[1312,128]{1,0:T(8,128)S(1)}, f32[8,512]{1,0:T(8,128)S(1)}) custom-call(f32[512,512]{1,0:T(8,128)S(1)} %get-tuple-element.91.diag_ref, f32[8,512]{1,0:T(8,128)S(1)} %pad.12.source_ref, f32[1,512]{1,0:T(1,128)S(1)} %broadcast_in_dim_reshape.3.across_ref), custom_call_target="tpu_custom_call" | custom-call | tf_op jit(solution)/shard_map/pallas_call | solution.py:228
  42.2 3.6 collective-permute-start
  45.9 8.2 %collective-permute-done.fall_ref = f32[1312,128]{1,0:T(8,128)S(1)} collective-permute-done((f32[1312,128]{1,0:T(8,128)S(1)}, f32[1312,128]{1,0:T(8,128)S(1)}, u32[]{:S(2)}, u32[]{:S(2)}) %collective-permute-start) | collective-permute-done | bytes 671776 | tf_op jit(solution)/shard_map/ppermute | solution.py:303
  54.1 41.0 %shard_map.66 = (f32[512,512]{1,0:T(8,128)S(1)}, f32[8,512]{1,0:T(8,128)S(1)}, f32[1312,128]{1,0:T(8,128)}, f32[1312,128]{1,0:T(8,128)}, f32[512,512]{1,0:T(8,12...) custom-call(s32[2]{0:T(128)S(1)} %add_convert_fusion.flag_ref, ...), custom_call_target="tpu_custom_call" | custom-call | tf_op jit(solution)/shard_map/pallas_call | solution.py:228
  97.4 1.6 collective-permute-start.4
  102.2 8.0 %collective-permute-done.2.fall_ref = f32[1312,128]{1,0:T(8,128)S(1)} collective-permute-done((f32[1312,128]{1,0:T(8,128)}, f32[1312,128]{1,0:T(8,128)S(1)}, u32[]{:S(2)}, u32[]{:S(2)}) %collective-permute-start.2) | collective-permute-done | bytes 671776 | tf_op jit(solution)/shard_map/ppermute | solution.py:303
  111.2 8.2 %shard_map.67 = (f32[512,512]{1,0:T(8,128)S(1)}, f32[8,512]{1,0:T(8,128)S(1)}, f32[1312,128]{1,0:T(8,128)}, f32[1312,128]{1,0:T(8,128)}, f32[512,512]{1,0:T(8,12...) custom-call(s32[2]{0:T(128)S(1)} %add_convert_fusion.1.flag_ref, f32[512,512]{1,0:T(8,128)} %copy-done.10, ...), custom_call_target="tpu_custom_call" | custom-call | tf_op jit(solution)/shard_map/pallas_call | solution.py:228
  120.4 1.7 collective-permute-start.7
  122.1 1.6 collective-permute-start.8
  129.1 8.5 %shard_map.68 = (f32[512,512]{1,0:T(8,128)S(1)}, f32[8,512]{1,0:T(8,128)S(1)}, f32[1312,128]{1,0:T(8,128)}, f32[1312,128]{1,0:T(8,128)}, f32[512,512]{1,0:T(8,12...) custom-call(s32[2]{0:T(128)S(1)} %add_convert_fusion.2.flag_ref, f32[512,512]{1,0:T(8,128)} %copy-done.8, ...), custom_call_target="tpu_custom_call" | custom-call | tf_op jit(solution)/shard_map/pallas_call | solution.py:228
  138.7 1.6 collective-permute-start.11
  140.3 1.6 collective-permute-start.12
  145.1 8.6 %shard_map.69 = (f32[512,512]{1,0:T(8,128)S(1)}, f32[8,512]{1,0:T(8,128)S(1)}, f32[1312,128]{1,0:T(8,128)}, f32[1312,128]{1,0:T(8,128)}, f32[512,512]{1,0:T(8,12...) custom-call(s32[2]{0:T(128)S(1)} %add_convert_fusion.3.flag_ref, f32[512,512]{1,0:T(8,128)} %copy-done.9, ...), custom_call_target="tpu_custom_call" | custom-call | tf_op jit(solution)/shard_map/pallas_call | solution.py:228
  155.7 1.6 collective-permute-start.15
  157.3 1.7 collective-permute-start.16
  162.1 14.2 %shard_map.70 = (f32[512,512]{1,0:T(8,128)S(1)}, f32[8,512]{1,0:T(8,128)S(1)}, f32[1312,128]{1,0:T(8,128)S(1)}, f32[1312,128]{1,0:T(8,128)}, f32[512,512]{1,0:T(...) custom-call(s32[2]{0:T(128)S(1)} %add_convert_fusion.4.flag_ref, ...), custom_call_target="tpu_custom_call" | custom-call | tf_op jit(solution)/shard_map/pallas_call | solution.py:228
  177.0 26.0 %shard_map.71.gains_ref = f32[8,512]{1,0:T(8,128)S(1)} custom-call(f32[512,512]{1,0:T(8,128)S(1)} %get-tuple-element.73.diag_ref, f32[1312,128]{1,0:T(8,128)S(1)} %collective-permute-done.17.rise_ref, f32[8,512]{1,0:T(8,128)S(1)} %get-tuple-element.75.source_ref), custom_call_target="tpu_custom_call" | custom-call | tf_op jit(solution)/shard_map/pallas_call | solution.py:228
  203.7 1.6 copy-done.6
  214.8 235.1 %collective-permute-done.25.below_ref = f32[8,512]{1,0:T(8,128)S(1)} collective-permute-done((f32[8,512]{1,0:T(8,128)S(1)}, f32[8,512]{1,0:T(8,128)S(1)}, u32[]{:S(2)}, u32[]{:S(2)}) %collective-permute-start.25) | collective-permute-done | bytes 16416 | tf_op jit(solution)/shard_map/ppermute | solution.py:303
  449.8 3.2 collective-permute-done.26.above_ref
  453.1 2.1 shard_map.76
  455.2 1.9 collective-permute-start.27
  457.1 4.9 %collective-permute-done.27 = f32[8,512]{1,0:T(8,128)S(1)} collective-permute-done((f32[8,512]{1,0:T(8,128)S(1)}, f32[8,512]{1,0:T(8,128)S(1)}, u32[]{:S(2)}, u32[]{:S(2)}) %collective-permute-start.27) | collective-permute-done | bytes 16416 | tf_op jit(solution)/shard_map/ppermute | solution.py:303
  (111 shorter events, 41.4 us)
Async XLA Ops:
  42.2 11.9 %collective-permute-start = (f32[1312,128]{1,0:T(8,128)S(1)}, f32[1312,128]{1,0:T(8,128)S(1)}, u32[]{:S(2)}, u32[]{:S(2)}) collective-permute-start(f32[1312,128]{1,0:T(8,128)S(1)} %get-tuple-element.51.rise_ref), channel_id=1, source_target_pairs={{1,0},{2,1},{3,2},{4,3},{5,4},{6,5},{7,6},{8,7},{9,8},{10,9},{11,1... | collective-permute-start | bytes 2015240 | tf_op jit(solution)/shard_map/ppermute | solution.py:303
  96.0 14.2 %collective-permute-start.3 = (f32[512,512]{1,0:T(8,128)}, f32[512,512]{1,0:T(8,128)S(1)}, u32[]{:S(2)}, u32[]{:S(2)}) collective-permute-start(f32[512,512]{1,0:T(8,128)} %get-tuple-element.56), channel_id=1, source_target_pairs={{0,1},{4,5},{8,9},{12,13},{16,17},{20,21},{24,25},{28,29}} | collective-permute-start | bytes 3145736 | tf_op jit(solution)/shard_map/ppermute | solution.py:303
  97.4 12.9 %collective-permute-start.4 = (f32[512,512]{1,0:T(8,128)}, f32[512,512]{1,0:T(8,128)}, u32[]{:S(2)}, u32[]{:S(2)}) collective-permute-start(f32[512,512]{1,0:T(8,128)} %get-tuple-element.56), channel_id=1, source_target_pairs={{2,1},{6,5},{10,9},{14,13},{18,17},{22,21},{26,25},{30,29}} | collective-permute-start | bytes 3145736 | tf_op jit(solution)/shard_map/ppermute | solution.py:303
  99.0 3.2 collective-permute-start.1
  100.3 9.9 %collective-permute-start.2 = (f32[1312,128]{1,0:T(8,128)}, f32[1312,128]{1,0:T(8,128)S(1)}, u32[]{:S(2)}, u32[]{:S(2)}) collective-permute-start(f32[1312,128]{1,0:T(8,128)} %get-tuple-element.55), channel_id=1, source_target_pairs={{2,1},{4,3},{6,5},{8,7},{10,9},{12,11},{14,13},{16,15},{18,17},{20... | collective-permute-start | bytes 2015240 | tf_op jit(solution)/shard_map/ppermute | solution.py:303
  120.4 6.5 %collective-permute-start.7 = (f32[512,512]{1,0:T(8,128)}, f32[512,512]{1,0:T(8,128)}, u32[]{:S(2)}, u32[]{:S(2)}) collective-permute-start(f32[512,512]{1,0:T(8,128)} %get-tuple-element.61), channel_id=1, source_target_pairs={{1,3},{9,11},{17,19},{25,27}} | collective-permute-start | bytes 3145736 | tf_op jit(solution)/shard_map/ppermute | solution.py:303
  122.1 4.8 %collective-permute-start.8 = (f32[512,512]{1,0:T(8,128)}, f32[512,512]{1,0:T(8,128)}, u32[]{:S(2)}, u32[]{:S(2)}) collective-permute-start(f32[512,512]{1,0:T(8,128)} %get-tuple-element.61), channel_id=1, source_target_pairs={{5,3},{13,11},{21,19},{29,27}} | collective-permute-start | bytes 3145736 | tf_op jit(solution)/shard_map/ppermute | solution.py:303
  123.7 1.5 collective-permute-start.5
  124.4 1.7 collective-permute-start.6
  138.7 6.4 %collective-permute-start.11 = (f32[512,512]{1,0:T(8,128)}, f32[512,512]{1,0:T(8,128)}, u32[]{:S(2)}, u32[]{:S(2)}) collective-permute-start(f32[512,512]{1,0:T(8,128)} %get-tuple-element.66), channel_id=1, source_target_pairs={{3,7},{19,23}} | collective-permute-start | bytes 3145736 | tf_op jit(solution)/shard_map/ppermute | solution.py:303
  140.3 4.7 %collective-permute-start.12 = (f32[512,512]{1,0:T(8,128)}, f32[512,512]{1,0:T(8,128)}, u32[]{:S(2)}, u32[]{:S(2)}) collective-permute-start(f32[512,512]{1,0:T(8,128)} %get-tuple-element.66), channel_id=1, source_target_pairs={{11,7},{27,23}} | collective-permute-start | bytes 3145736 | tf_op jit(solution)/shard_map/ppermute | solution.py:303
  142.0 3.1 collective-permute-start.10
  143.5 1.6 collective-permute-start.9
  155.7 6.4 %collective-permute-start.15 = (f32[512,512]{1,0:T(8,128)}, f32[512,512]{1,0:T(8,128)}, u32[]{:S(2)}, u32[]{:S(2)}) collective-permute-start(f32[512,512]{1,0:T(8,128)} %get-tuple-element.71), channel_id=1, source_target_pairs={{7,15}} | collective-permute-start | bytes 3145736 | tf_op jit(solution)/shard_map/ppermute | solution.py:303
  157.3 4.8 %collective-permute-start.16 = (f32[512,512]{1,0:T(8,128)}, f32[512,512]{1,0:T(8,128)}, u32[]{:S(2)}, u32[]{:S(2)}) collective-permute-start(f32[512,512]{1,0:T(8,128)} %get-tuple-element.71), channel_id=1, source_target_pairs={{23,15}} | collective-permute-start | bytes 3145736 | tf_op jit(solution)/shard_map/ppermute | solution.py:303
  158.9 3.1 collective-permute-start.13
  160.4 1.6 collective-permute-start.14
  176.3 0.7 collective-permute-start.17
  205.8 1.5 collective-permute-start.19
  207.9 1.5 collective-permute-start.21
  210.0 1.5 collective-permute-start.23
  212.1 237.8 %collective-permute-start.25 = (f32[8,512]{1,0:T(8,128)S(1)}, f32[8,512]{1,0:T(8,128)S(1)}, u32[]{:S(2)}, u32[]{:S(2)}) collective-permute-start(f32[8,512]{1,0:T(8,128)S(1)} %shard_map.75.gains_ref), channel_id=1, source_target_pairs={{1,2},{3,4},{5,6},{7,8},{9,10},{11,12},{13,14},{15,16},{17,18},{19... | collective-permute-start | bytes 49160 | tf_op jit(solution)/shard_map/ppermute | solution.py:303
  213.5 239.6 %collective-permute-start.26 = (f32[8,512]{1,0:T(8,128)S(1)}, f32[8,512]{1,0:T(8,128)S(1)}, u32[]{:S(2)}, u32[]{:S(2)}) collective-permute-start(f32[8,512]{1,0:T(8,128)S(1)} %shard_map.75.gains_ref), channel_id=1, source_target_pairs={{1,0},{3,2},{5,4},{7,6},{9,8},{11,10},{13,12},{15,14},{17,16},{19,... | collective-permute-start | bytes 49160 | tf_op jit(solution)/shard_map/ppermute | solution.py:303
  455.2 6.9 %collective-permute-start.27 = (f32[8,512]{1,0:T(8,128)S(1)}, f32[8,512]{1,0:T(8,128)S(1)}, u32[]{:S(2)}, u32[]{:S(2)}) collective-permute-start(f32[8,512]{1,0:T(8,128)S(1)} %shard_map.76), channel_id=1, source_target_pairs={{0,1},{1,2},{2,3},{3,4},{4,5},{5,6},{6,7},{7,8},{8,9},{9,10},{10,1... | collective-permute-start | bytes 49160 | tf_op jit(solution)/shard_map/ppermute | solution.py:303
  (25 other events, 593.4 us)

commit v2 on v1

--- a/solution.py
+++ b/solution.py
@@ -10,8 +10,9 @@
 ridge_weight = 1.0
 PANEL = 128
 SUB = 8
-PIVOTS = 4
+PIVOTS = 8
 BLK = 32
+VMEM_LIMIT = 28 << 20
 HIGHEST = lax.Precision.HIGHEST
 
 
@@ -153,7 +154,9 @@
         x_ref[cut(r), (r + 1) * PANEL :] = jnp.zeros((PANEL, width - (r + 1) * PANEL), jnp.float32)
 
 
-def first_kernel(diag_ref, source_ref, across_ref, coupling_ref, packed_ref, y_ref, x_ref, t_ref):
+def first_kernel(
+    diag_ref, source_ref, across_ref, coupling_ref, packed_ref, y_ref, c_ref, line_ref, x_ref, t_ref
+):
     width = diag_ref.shape[0]
     x_ref[...] = diag_ref[...]
     factor(x_ref)
@@ -172,9 +175,9 @@
 
 def level_kernel(first, flag_ref, diag_ref, rise_ref, fall_ref, below_ref, *refs):
     if first:
-        source_ref, *outs, above_ref = refs
+        source_ref, _, _, _, *outs, above_ref = refs
     else:
-        above_ref, source_ref, *outs = refs
+        above_ref, source_ref, _, _, _, *outs = refs
     diag_out, source_out, up_ref, down_ref, cross_ref, c_ref, line_ref, x_ref = outs
     width = diag_ref.shape[0]
     for r, c, at in pairs(width):
@@ -222,7 +225,7 @@
         out_ref[...] = mm(line, x_ref[...])
 
 
-def call(kernel, outs, *operands, scratch=()):
+def call(kernel, outs, *operands, scratch=(), aliases=None):
     vmem = pl.BlockSpec(memory_space=pltpu.VMEM)
     smem = pl.BlockSpec(memory_space=pltpu.SMEM)
     return pl.pallas_call(
@@ -231,7 +234,8 @@
         in_specs=[smem if o.dtype == jnp.int32 else vmem for o in operands],
         out_specs=[vmem] * len(outs),
         scratch_shapes=[pltpu.VMEM(s, jnp.float32) for s in scratch],
-        compiler_params=pltpu.CompilerParams(vmem_limit_bytes=48 << 20),
+        input_output_aliases=aliases or {},
+        compiler_params=pltpu.CompilerParams(vmem_limit_bytes=VMEM_LIMIT),
     )(*operands)
 
 def normal_kernel(vis_ref, obs_ref, keep_ref, one_ref, two_ref, normal_ref, target_ref):
@@ -334,9 +338,9 @@
     def as_line(vector):
         return jnp.pad(vector[None, :], ((0, SUB - 1), (0, 0)))
 
-    coupling, rise, y0 = call(
-        first_kernel, (square, packed, line),
-        diagonal(0), as_line(targets[0]), smooth[None, :], scratch=(square, square),
+    coupling, rise, y0, c, solved, inverse = call(
+        first_kernel, (square, packed, line, (2,) + square, line, square),
+        diagonal(0), as_line(targets[0]), smooth[None, :], scratch=(square,),
     )
     fall = move(rise, [(i, i - 1) for i in range(1, devices)])
     diag, source, below, above = diagonal(1), as_line(targets[1]), coupling, None
@@ -353,9 +357,11 @@
         diag, source, up, down, cross, c, solved, inverse = call(
             functools.partial(level_kernel, level == 0),
             (square, line, packed, packed, square, (2,) + square, line, square),
-            flag, diag, rise, fall, *sides, source, scratch=(square,) * (level == 0),
+            flag, diag, rise, fall, *sides, source, c, solved, inverse,
+            scratch=(square,) * (level == 0),
+            aliases={1: 0, len(sides) + 4: 1, len(sides) + 5: 5, len(sides) + 6: 6, len(sides) + 7: 7},
         )
-        kept.append((flag, c, solved, inverse))
+        kept.append(flag)
         gone = range(stride - 1, devices, 2 * stride)
         rises = [(i, i + stride) for i in gone]
         falls = [(i, i - stride) for i in gone if i >= stride]
@@ -369,7 +375,7 @@
     (gains,) = call(last_kernel, (line,), diag, rise, source, scratch=(square,))
     for level in reversed(range(levels)):
         stride = 1 << level
-        flag, c, solved, inverse = kept[level]
+        flag = kept[level]
         gone = range(stride - 1, devices, 2 * stride)
         from_above = move(gains, [(i + stride, i) for i in gone])
         falling = [(i - stride, i) for i in gone if i >= stride]

time: 470 us -> 433 us (0.921)
  waiting for transfers between devices: 260 us -> 236 us
  Pallas kernels: 146 us -> 128 us
    ppermute x28, waiting for transfers between devices: 260 us -> 236 us  [move(): return lax.ppermute(block, 'freq', route)]
    pallas_call x12, Pallas kernels: 138 us -> 120 us  [call(): pl.pallas_call(kernel, out_shape=[jax.ShapeDtypeStruct(o, jnp.float32) fo...]
    unnamed x42 -> x30, local copies, waits for them, and re-layouts: 14.8 us -> 14.6 us
  transfers between devices with their start and end apart: 28 -> 28, of which waited for: 6 -> 5; matrix products, arithmetic and copies ran while one was open for 0% -> 0% of each run, Pallas kernels for 0% -> 0%
where the time goes in v2:
time: 433 us; the launch traced here: 426 us
  waiting for transfers between devices  236 us (55%)
  Pallas kernels  128 us (30%)
  starting transfers between devices  40.8 us (9%)
  local copies, waits for them, and re-layouts  17.9 us (4%)
    ppermute x28, waiting for transfers between devices, move(): return lax.ppermute(block, 'freq', route)  236 us
    pallas_call x12, Pallas kernels, call(): pl.pallas_call(kernel, out_shape=[jax.ShapeDtypeStruct(o, jnp.float32) fo...  120 us
    ppermute x28, starting transfers between devices, move(): return lax.ppermute(block, 'freq', route)  40.8 us
    unnamed x30, local copies, waits for them, and re-layouts  14.6 us
  transfers between devices with their start and end apart: 28, of which 5 were waited for; matrix products, arithmetic and copies ran while one was open for 0% of the time, Pallas kernels for 0%

profile of v2, /device:TPU:8, one launch (start us, length us, event | category | flops | bytes accessed | tf_op | source)
XLA Modules:
  0.0 426.2 jit_solution(2046744273783211332)
XLA Ops:
  4.8 7.8 %shard_map.64 = (f32[2,512,512]{2,1,0:T(8,128)S(1)}, f32[2,8,512]{2,1,0:T(8,128)S(1)}) custom-call(bf16[2,8,4096]{2,1,0:T(8,128)(2,1)S(1)} %copy-done.12, f32[2,1,4096]{2,1,0:T(1,128)S(1)} %reshape.47.obs_ref, s32[2,1,4096]{2,1,0:T(1,128)S(1)} %reshape.48.keep_ref, s32[1,4096]{1,0:T(1,128)S(1)} %bitcast.18, s32[1,4096]{1,0:T(1,128)S(1)} %bitcast.19), custom_call_target="tpu_custom_call" | custom-call | tf_op jit(solution)/shard_map/pallas_call | solution.py:278
  14.1 22.6 %shard_map.65 = (f32[512,512]{1,0:T(8,128)S(1)}, f32[1312,128]{1,0:T(8,128)}, f32[8,512]{1,0:T(8,128)S(1)}, f32[2,512,512]{2,1,0:T(8,128)S(1)}, f32[8,512]{1,0:T(8,128)S(1)}, /*index=5*/f32[512,512]{1,0:T(8,128)S(1)}) custom-call(f32[512,512]{1,0:T(8,128)S(1)} %get-tuple-element.97.diag_ref, f32[8,512]{1,0:T(8,128)S(1)} %pad.12.source_ref, ...), custom_call_target="tpu_custom_call" | custom-call | tf_op jit(solution)/shard_map/pallas_call | solution.py:231
  37.7 3.7 collective-permute-start
  41.5 8.5 %collective-permute-done.fall_ref = f32[1312,128]{1,0:T(8,128)} collective-permute-done((f32[1312,128]{1,0:T(8,128)}, f32[1312,128]{1,0:T(8,128)}, u32[]{:S(2)}, u32[]{:S(2)}) %collective-permute-start) | collective-permute-done | bytes 671776 | tf_op jit(solution)/shard_map/ppermute | solution.py:307
  52.5 34.9 %shard_map.66 = (f32[512,512]{1,0:T(8,128)S(1)}, f32[8,512]{1,0:T(8,128)S(1)}, f32[1312,128]{1,0:T(8,128)}, f32[1312,128]{1,0:T(8,128)}, f32[512,512]{1,0:T(8,12...) custom-call(s32[2]{0:T(128)S(1)} %add_convert_fusion.flag_ref, ...), custom_call_target="tpu_custom_call", output_to_operand_aliasing={{0}: (1, {}), {1}: (5, {}), {5}: (6, {}), {6}: (7, {}), {7}... | custom-call | tf_op jit(solution)/shard_map/pallas_call | solution.py:231
  88.3 2.3 collective-permute-start.3
  90.6 1.6 collective-permute-start.4
  92.2 2.1 collective-permute-start.1
  94.3 2.2 collective-permute-start.2
  96.6 7.6 %collective-permute-done.2.fall_ref = f32[1312,128]{1,0:T(8,128)} collective-permute-done((f32[1312,128]{1,0:T(8,128)}, f32[1312,128]{1,0:T(8,128)}, u32[]{:S(2)}, u32[]{:S(2)}) %collective-permute-start.2) | collective-permute-done | bytes 671776 | tf_op jit(solution)/shard_map/ppermute | solution.py:307
  105.4 8.3 %shard_map.67 = (f32[512,512]{1,0:T(8,128)S(1)}, f32[8,512]{1,0:T(8,128)S(1)}, f32[1312,128]{1,0:T(8,128)}, f32[1312,128]{1,0:T(8,128)}, f32[512,512]{1,0:T(8,12...) custom-call(s32[2]{0:T(128)S(1)} %add_convert_fusion.1.flag_ref, ...), custom_call_target="tpu_custom_call", output_to_operand_aliasing={{0}: (1, {}), {1}: (6, {}), {5}: (7, {}), {6}: (8, {}), {7}... | custom-call | tf_op jit(solution)/shard_map/pallas_call | solution.py:231
  114.7 1.6 collective-permute-start.7
  116.3 1.6 collective-permute-start.8
  122.3 8.0 %shard_map.68 = (f32[512,512]{1,0:T(8,128)S(1)}, f32[8,512]{1,0:T(8,128)S(1)}, f32[1312,128]{1,0:T(8,128)}, f32[1312,128]{1,0:T(8,128)}, f32[512,512]{1,0:T(8,12...) custom-call(s32[2]{0:T(128)S(1)} %add_convert_fusion.2.flag_ref, ...), custom_call_target="tpu_custom_call", output_to_operand_aliasing={{0}: (1, {}), {1}: (6, {}), {5}: (7, {}), {6}: (8, {}), {7}... | custom-call | tf_op jit(solution)/shard_map/pallas_call | solution.py:231
  133.0 1.6 collective-permute-start.12
  139.0 8.3 %shard_map.69 = (f32[512,512]{1,0:T(8,128)S(1)}, f32[8,512]{1,0:T(8,128)S(1)}, f32[1312,128]{1,0:T(8,128)}, f32[1312,128]{1,0:T(8,128)}, f32[512,512]{1,0:T(8,12...) custom-call(s32[2]{0:T(128)S(1)} %add_convert_fusion.3.flag_ref, ...), custom_call_target="tpu_custom_call", output_to_operand_aliasing={{0}: (1, {}), {1}: (6, {}), {5}: (7, {}), {6}: (8, {}), {7}... | custom-call | tf_op jit(solution)/shard_map/pallas_call | solution.py:231
  149.9 1.6 collective-permute-start.16
  155.9 13.3 %shard_map.70 = (f32[512,512]{1,0:T(8,128)S(1)}, f32[8,512]{1,0:T(8,128)S(1)}, f32[1312,128]{1,0:T(8,128)S(1)}, f32[1312,128]{1,0:T(8,128)}, f32[512,512]{1,0:T(...) custom-call(s32[2]{0:T(128)S(1)} %add_convert_fusion.4.flag_ref, ...), custom_call_target="tpu_custom_call", output_to_operand_aliasing={{0}: (1, {}), {1}: (6, {}), {5}: (7, {}), {6}: (8, {}), {7}... | custom-call | tf_op jit(solution)/shard_map/pallas_call | solution.py:231
  169.9 20.8 %shard_map.71.gains_ref = f32[8,512]{1,0:T(8,128)S(1)} custom-call(f32[512,512]{1,0:T(8,128)S(1)} %get-tuple-element.91.diag_ref, f32[1312,128]{1,0:T(8,128)S(1)} %collective-permute-done.17.rise_ref, f32[8,512]{1,0:T(8,128)S(1)} %get-tuple-element.93.source_ref), custom_call_target="tpu_custom_call" | custom-call | tf_op jit(solution)/shard_map/pallas_call | solution.py:231
  200.5 212.0 %collective-permute-done.25.below_ref = f32[8,512]{1,0:T(8,128)S(1)} collective-permute-done((f32[8,512]{1,0:T(8,128)S(1)}, f32[8,512]{1,0:T(8,128)S(1)}, u32[]{:S(2)}, u32[]{:S(2)}) %collective-permute-start.25) | collective-permute-done | bytes 16416 | tf_op jit(solution)/shard_map/ppermute | solution.py:307
  412.4 3.2 collective-permute-done.26.above_ref
  415.6 2.1 shard_map.76
  417.7 1.9 collective-permute-start.27
  419.7 4.9 %collective-permute-done.27 = f32[8,512]{1,0:T(8,128)S(1)} collective-permute-done((f32[8,512]{1,0:T(8,128)S(1)}, f32[8,512]{1,0:T(8,128)S(1)}, u32[]{:S(2)}, u32[]{:S(2)}) %collective-permute-start.27) | collective-permute-done | bytes 16416 | tf_op jit(solution)/shard_map/ppermute | solution.py:307
  (99 shorter events, 43.0 us)
Async XLA Ops:
  37.7 12.3 %collective-permute-start = (f32[1312,128]{1,0:T(8,128)}, f32[1312,128]{1,0:T(8,128)}, u32[]{:S(2)}, u32[]{:S(2)}) collective-permute-start(f32[1312,128]{1,0:T(8,128)} %get-tuple-element.54.rise_ref), channel_id=1, source_target_pairs={{1,0},{2,1},{3,2},{4,3},{5,4},{6,5},{7,6},{8,7},{9,8},{10,9},{11,1... | collective-permute-start | bytes 2015240 | tf_op jit(solution)/shard_map/ppermute | solution.py:307
  88.3 15.9 %collective-permute-start.3 = (f32[512,512]{1,0:T(8,128)}, f32[512,512]{1,0:T(8,128)}, u32[]{:S(2)}, u32[]{:S(2)}) collective-permute-start(f32[512,512]{1,0:T(8,128)} %get-tuple-element.62), channel_id=1, source_target_pairs={{0,1},{4,5},{8,9},{12,13},{16,17},{20,21},{24,25},{28,29}} | collective-permute-start | bytes 3145736 | tf_op jit(solution)/shard_map/ppermute | solution.py:307
  90.6 13.6 %collective-permute-start.4 = (f32[512,512]{1,0:T(8,128)}, f32[512,512]{1,0:T(8,128)}, u32[]{:S(2)}, u32[]{:S(2)}) collective-permute-start(f32[512,512]{1,0:T(8,128)} %get-tuple-element.62), channel_id=1, source_target_pairs={{2,1},{6,5},{10,9},{14,13},{18,17},{22,21},{26,25},{30,29}} | collective-permute-start | bytes 3145736 | tf_op jit(solution)/shard_map/ppermute | solution.py:307
  92.2 4.4 %collective-permute-start.1 = (f32[1312,128]{1,0:T(8,128)}, f32[1312,128]{1,0:T(8,128)}, u32[]{:S(2)}, u32[]{:S(2)}) collective-permute-start(f32[1312,128]{1,0:T(8,128)} %get-tuple-element.60), channel_id=1, source_target_pairs={{0,1},{2,3},{4,5},{6,7},{8,9},{10,11},{12,13},{14,15},{16,17},{18,... | collective-permute-start | bytes 2015240 | tf_op jit(solution)/shard_map/ppermute | solution.py:307
  94.3 9.9 %collective-permute-start.2 = (f32[1312,128]{1,0:T(8,128)}, f32[1312,128]{1,0:T(8,128)}, u32[]{:S(2)}, u32[]{:S(2)}) collective-permute-start(f32[1312,128]{1,0:T(8,128)} %get-tuple-element.61), channel_id=1, source_target_pairs={{2,1},{4,3},{6,5},{8,7},{10,9},{12,11},{14,13},{16,15},{18,17},{20... | collective-permute-start | bytes 2015240 | tf_op jit(solution)/shard_map/ppermute | solution.py:307
  114.7 6.4 %collective-permute-start.7 = (f32[512,512]{1,0:T(8,128)}, f32[512,512]{1,0:T(8,128)}, u32[]{:S(2)}, u32[]{:S(2)}) collective-permute-start(f32[512,512]{1,0:T(8,128)} %get-tuple-element.70), channel_id=1, source_target_pairs={{1,3},{9,11},{17,19},{25,27}} | collective-permute-start | bytes 3145736 | tf_op jit(solution)/shard_map/ppermute | solution.py:307
  116.3 4.8 %collective-permute-start.8 = (f32[512,512]{1,0:T(8,128)}, f32[512,512]{1,0:T(8,128)}, u32[]{:S(2)}, u32[]{:S(2)}) collective-permute-start(f32[512,512]{1,0:T(8,128)} %get-tuple-element.70), channel_id=1, source_target_pairs={{5,3},{13,11},{21,19},{29,27}} | collective-permute-start | bytes 3145736 | tf_op jit(solution)/shard_map/ppermute | solution.py:307
  118.0 3.1 collective-permute-start.5
  119.5 1.6 collective-permute-start.6
  131.4 6.4 %collective-permute-start.11 = (f32[512,512]{1,0:T(8,128)}, f32[512,512]{1,0:T(8,128)}, u32[]{:S(2)}, u32[]{:S(2)}) collective-permute-start(f32[512,512]{1,0:T(8,128)} %get-tuple-element.78), channel_id=1, source_target_pairs={{3,7},{19,23}} | collective-permute-start | bytes 3145736 | tf_op jit(solution)/shard_map/ppermute | solution.py:307
  133.0 4.8 %collective-permute-start.12 = (f32[512,512]{1,0:T(8,128)}, f32[512,512]{1,0:T(8,128)}, u32[]{:S(2)}, u32[]{:S(2)}) collective-permute-start(f32[512,512]{1,0:T(8,128)} %get-tuple-element.78), channel_id=1, source_target_pairs={{11,7},{27,23}} | collective-permute-start | bytes 3145736 | tf_op jit(solution)/shard_map/ppermute | solution.py:307
  134.6 3.1 collective-permute-start.10
  136.2 1.6 collective-permute-start.9
  148.3 6.4 %collective-permute-start.15 = (f32[512,512]{1,0:T(8,128)}, f32[512,512]{1,0:T(8,128)}, u32[]{:S(2)}, u32[]{:S(2)}) collective-permute-start(f32[512,512]{1,0:T(8,128)} %get-tuple-element.86), channel_id=1, source_target_pairs={{7,15}} | collective-permute-start | bytes 3145736 | tf_op jit(solution)/shard_map/ppermute | solution.py:307
  149.9 4.8 %collective-permute-start.16 = (f32[512,512]{1,0:T(8,128)}, f32[512,512]{1,0:T(8,128)}, u32[]{:S(2)}, u32[]{:S(2)}) collective-permute-start(f32[512,512]{1,0:T(8,128)} %get-tuple-element.86), channel_id=1, source_target_pairs={{23,15}} | collective-permute-start | bytes 3145736 | tf_op jit(solution)/shard_map/ppermute | solution.py:307
  151.6 3.1 collective-permute-start.13
  153.0 1.6 collective-permute-start.14
  169.2 0.7 collective-permute-start.17
  192.0 1.3 collective-permute-start.19
  193.9 1.3 collective-permute-start.21
  195.8 1.3 collective-permute-start.23
  197.7 214.7 %collective-permute-start.25 = (f32[8,512]{1,0:T(8,128)S(1)}, f32[8,512]{1,0:T(8,128)S(1)}, u32[]{:S(2)}, u32[]{:S(2)}) collective-permute-start(f32[8,512]{1,0:T(8,128)S(1)} %shard_map.75.gains_ref), channel_id=1, source_target_pairs={{1,2},{3,4},{5,6},{7,8},{9,10},{11,12},{13,14},{15,16},{17,18},{19... | collective-permute-start | bytes 49160 | tf_op jit(solution)/shard_map/ppermute | solution.py:307
  199.2 216.5 %collective-permute-start.26 = (f32[8,512]{1,0:T(8,128)S(1)}, f32[8,512]{1,0:T(8,128)S(1)}, u32[]{:S(2)}, u32[]{:S(2)}) collective-permute-start(f32[8,512]{1,0:T(8,128)S(1)} %shard_map.75.gains_ref), channel_id=1, source_target_pairs={{1,0},{3,2},{5,4},{7,6},{9,8},{11,10},{13,12},{15,14},{17,16},{19,... | collective-permute-start | bytes 49160 | tf_op jit(solution)/shard_map/ppermute | solution.py:307
  417.7 6.9 %collective-permute-start.27 = (f32[8,512]{1,0:T(8,128)S(1)}, f32[8,512]{1,0:T(8,128)S(1)}, u32[]{:S(2)}, u32[]{:S(2)}) collective-permute-start(f32[8,512]{1,0:T(8,128)S(1)} %shard_map.76), channel_id=1, source_target_pairs={{0,1},{1,2},{2,3},{3,4},{4,5},{5,6},{6,7},{7,8},{8,9},{9,10},{10,1... | collective-permute-start | bytes 49160 | tf_op jit(solution)/shard_map/ppermute | solution.py:307
  (19 other events, 244.2 us)

commit v3 on v2

--- a/solution.py
+++ b/solution.py
@@ -12,7 +12,7 @@
 SUB = 8
 PIVOTS = 8
 BLK = 32
-VMEM_LIMIT = 28 << 20
+VMEM_LIMIT = 24 << 20
 HIGHEST = lax.Precision.HIGHEST
 
 
@@ -175,10 +175,11 @@
 
 def level_kernel(first, flag_ref, diag_ref, rise_ref, fall_ref, below_ref, *refs):
     if first:
-        source_ref, _, _, _, *outs, above_ref = refs
+        source_ref, _, _, _, *outs = refs
     else:
         above_ref, source_ref, _, _, _, *outs = refs
-    diag_out, source_out, up_ref, down_ref, cross_ref, c_ref, line_ref, x_ref = outs
+    diag_out, source_out, up_out, down_out, cross_out, c_ref, line_ref, x_ref, *holds = outs
+    below_hold, above_hold, up_ref, down_ref, cross_ref, sems = holds
     width = diag_ref.shape[0]
     for r, c, at in pairs(width):
         diag_out[cut(r), cut(c)] = (
@@ -188,23 +189,40 @@
 
     @pl.when(flag_ref[0] == 1)
     def _():
+        loads = [pltpu.make_async_copy(below_ref, below_hold, sems.at[0])]
         if first:
-            fill_square(above_ref, fall_ref)
+            fill_square(above_hold, fall_ref)
+        else:
+            loads.append(pltpu.make_async_copy(above_ref, above_hold, sems.at[1]))
+        for load in loads:
+            load.start()
         x_ref[...] = diag_out[...]
         factor(x_ref)
+        for load in loads:
+            load.wait()
         half = width // 2
-        for side, ref in enumerate((below_ref, above_ref)):
+        for side, ref in enumerate((below_hold, above_hold)):
             c_ref[side, :, :half] = mm(ref[:, :half], x_ref[:half, :half], NT)
             c_ref[side, :, half:] = mm(ref[...], x_ref[half:, :], NT)
         line = mm(source_out[...], x_ref[...], NT)
         line_ref[...] = line
         cross_ref[...] = mm(c_ref[flag_ref[1]], c_ref[1 - flag_ref[1]], NT)
+        stores = [
+            pltpu.make_async_copy(ref, out, sems.at[2 + i])
+            for i, (ref, out) in enumerate(
+                ((cross_ref, cross_out), (down_ref, down_out), (up_ref, up_out))
+            )
+        ]
+        stores[0].start()
         for side, ref in enumerate((down_ref, up_ref)):
             put_line(ref, mm(line, c_ref[side], NT))
             for r in range(width // PANEL):
                 value = mm(c_ref[side, cut(r), :], c_ref[side, : (r + 1) * PANEL, :], NT)
                 for c in range(r + 1):
                     ref[cut(r * (r + 1) // 2 + c), :] = value[:, cut(c)]
+            stores[1 + side].start()
+        for store in stores:
+            store.wait()
 
 
 def last_kernel(diag_ref, rise_ref, source_ref, y_ref, x_ref):
@@ -225,15 +243,19 @@
         out_ref[...] = mm(line, x_ref[...])
 
 
-def call(kernel, outs, *operands, scratch=(), aliases=None):
+def call(kernel, outs, *operands, scratch=(), aliases=None, far_in=(), far_out=(), sems=()):
     vmem = pl.BlockSpec(memory_space=pltpu.VMEM)
     smem = pl.BlockSpec(memory_space=pltpu.SMEM)
+    far = pl.BlockSpec(memory_space=pl.ANY)
     return pl.pallas_call(
         kernel,
         out_shape=[jax.ShapeDtypeStruct(o, jnp.float32) for o in outs],
-        in_specs=[smem if o.dtype == jnp.int32 else vmem for o in operands],
-        out_specs=[vmem] * len(outs),
-        scratch_shapes=[pltpu.VMEM(s, jnp.float32) for s in scratch],
+        in_specs=[
+            smem if o.dtype == jnp.int32 else far if i in far_in else vmem
+            for i, o in enumerate(operands)
+        ],
+        out_specs=[far if i in far_out else vmem for i in range(len(outs))],
+        scratch_shapes=[pltpu.VMEM(s, jnp.float32) for s in scratch] + list(sems),
         input_output_aliases=aliases or {},
         compiler_params=pltpu.CompilerParams(vmem_limit_bytes=VMEM_LIMIT),
     )(*operands)
@@ -358,7 +380,10 @@
             functools.partial(level_kernel, level == 0),
             (square, line, packed, packed, square, (2,) + square, line, square),
             flag, diag, rise, fall, *sides, source, c, solved, inverse,
-            scratch=(square,) * (level == 0),
+            scratch=(square, square, packed, packed, square),
+            far_in=range(4, 4 + len(sides)),
+            far_out=(2, 3, 4),
+            sems=(pltpu.SemaphoreType.DMA((5,)),),
             aliases={1: 0, len(sides) + 4: 1, len(sides) + 5: 5, len(sides) + 6: 6, len(sides) + 7: 7},
         )
         kept.append(flag)

time: 433 us -> 429 us (level)
  Pallas kernels: 128 us -> 120 us
    pallas_call x12, Pallas kernels: 120 us -> 112 us  [call(): pl.pallas_call(kernel, out_shape=[jax.ShapeDtypeStruct(o, jnp.float32) fo...]
where the time goes in v3:
time: 429 us; the launch traced here: 421 us
  waiting for transfers between devices  239 us (56%)
  Pallas kernels  120 us (28%)
  starting transfers between devices  40.8 us (10%)
  local copies, waits for them, and re-layouts  17.9 us (4%)
    ppermute x28, waiting for transfers between devices, move(): return lax.ppermute(block, 'freq', route)  239 us
    pallas_call x12, Pallas kernels, call(): pl.pallas_call(kernel, out_shape=[jax.ShapeDtypeStruct(o, jnp.float32) fo...  112 us
    ppermute x28, starting transfers between devices, move(): return lax.ppermute(block, 'freq', route)  40.8 us
    unnamed x30, local copies, waits for them, and re-layouts  14.6 us
  transfers between devices with their start and end apart: 28, of which 5 were waited for; matrix products, arithmetic and copies ran while one was open for 0% of the time, Pallas kernels for 0%

profile of v3, /device:TPU:8, one launch (start us, length us, event | category | flops | bytes accessed | tf_op | source)
XLA Modules:
  0.0 421.4 jit_solution(17002478264926629139)
XLA Ops:
  4.8 7.8 %shard_map.64 = (f32[2,512,512]{2,1,0:T(8,128)S(1)}, f32[2,8,512]{2,1,0:T(8,128)S(1)}) custom-call(bf16[2,8,4096]{2,1,0:T(8,128)(2,1)S(1)} %copy-done.12, f32[2,1,4096]{2,1,0:T(1,128)S(1)} %reshape.47.obs_ref, s32[2,1,4096]{2,1,0:T(1,128)S(1)} %reshape.48.keep_ref, s32[1,4096]{1,0:T(1,128)S(1)} %bitcast.18, s32[1,4096]{1,0:T(1,128)S(1)} %bitcast.19), custom_call_target="tpu_custom_call" | custom-call | tf_op jit(solution)/shard_map/pallas_call | solution.py:300
  14.1 22.6 %shard_map.65 = (f32[512,512]{1,0:T(8,128)S(1)}, f32[1312,128]{1,0:T(8,128)}, f32[8,512]{1,0:T(8,128)S(1)}, f32[2,512,512]{2,1,0:T(8,128)S(1)}, f32[8,512]{1,0:T(8,128)S(1)}, /*index=5*/f32[512,512]{1,0:T(8,128)S(1)}) custom-call(f32[512,512]{1,0:T(8,128)S(1)} %get-tuple-element.97.diag_ref, f32[8,512]{1,0:T(8,128)S(1)} %pad.12.source_ref, ...), custom_call_target="tpu_custom_call" | custom-call | tf_op jit(solution)/shard_map/pallas_call | solution.py:250
  37.7 3.7 collective-permute-start
  41.5 8.5 %collective-permute-done.fall_ref = f32[1312,128]{1,0:T(8,128)} collective-permute-done((f32[1312,128]{1,0:T(8,128)}, f32[1312,128]{1,0:T(8,128)}, u32[]{:S(2)}, u32[]{:S(2)}) %collective-permute-start) | collective-permute-done | bytes 671776 | tf_op jit(solution)/shard_map/ppermute | solution.py:329
  52.5 34.5 %shard_map.66 = (f32[512,512]{1,0:T(8,128)S(1)}, f32[8,512]{1,0:T(8,128)S(1)}, f32[1312,128]{1,0:T(8,128)}, f32[1312,128]{1,0:T(8,128)}, f32[512,512]{1,0:T(8,12...) custom-call(s32[2]{0:T(128)S(1)} %add_convert_fusion.flag_ref, ...), custom_call_target="tpu_custom_call", output_to_operand_aliasing={{0}: (1, {}), {1}: (5, {}), {5}: (6, {}), {6}: (7, {}), {7}... | custom-call | tf_op jit(solution)/shard_map/pallas_call | solution.py:250
  88.0 2.3 collective-permute-start.3
  90.2 1.6 collective-permute-start.4
  91.9 2.1 collective-permute-start.1
  94.0 2.2 collective-permute-start.2
  96.3 7.6 %collective-permute-done.2.fall_ref = f32[1312,128]{1,0:T(8,128)} collective-permute-done((f32[1312,128]{1,0:T(8,128)}, f32[1312,128]{1,0:T(8,128)}, u32[]{:S(2)}, u32[]{:S(2)}) %collective-permute-start.2) | collective-permute-done | bytes 671776 | tf_op jit(solution)/shard_map/ppermute | solution.py:329
  105.1 6.3 %shard_map.67 = (f32[512,512]{1,0:T(8,128)S(1)}, f32[8,512]{1,0:T(8,128)S(1)}, f32[1312,128]{1,0:T(8,128)}, f32[1312,128]{1,0:T(8,128)}, f32[512,512]{1,0:T(8,12...) custom-call(s32[2]{0:T(128)S(1)} %add_convert_fusion.1.flag_ref, ...), custom_call_target="tpu_custom_call", output_to_operand_aliasing={{0}: (1, {}), {1}: (6, {}), {5}: (7, {}), {6}: (8, {}), {7}... | custom-call | tf_op jit(solution)/shard_map/pallas_call | solution.py:250
  112.4 1.6 collective-permute-start.7
  114.0 1.6 collective-permute-start.8
  120.0 6.0 %shard_map.68 = (f32[512,512]{1,0:T(8,128)S(1)}, f32[8,512]{1,0:T(8,128)S(1)}, f32[1312,128]{1,0:T(8,128)}, f32[1312,128]{1,0:T(8,128)}, f32[512,512]{1,0:T(8,12...) custom-call(s32[2]{0:T(128)S(1)} %add_convert_fusion.2.flag_ref, ...), custom_call_target="tpu_custom_call", output_to_operand_aliasing={{0}: (1, {}), {1}: (6, {}), {5}: (7, {}), {6}: (8, {}), {7}... | custom-call | tf_op jit(solution)/shard_map/pallas_call | solution.py:250
  128.7 1.6 collective-permute-start.12
  134.7 6.3 %shard_map.69 = (f32[512,512]{1,0:T(8,128)S(1)}, f32[8,512]{1,0:T(8,128)S(1)}, f32[1312,128]{1,0:T(8,128)}, f32[1312,128]{1,0:T(8,128)}, f32[512,512]{1,0:T(8,12...) custom-call(s32[2]{0:T(128)S(1)} %add_convert_fusion.3.flag_ref, ...), custom_call_target="tpu_custom_call", output_to_operand_aliasing={{0}: (1, {}), {1}: (6, {}), {5}: (7, {}), {6}: (8, {}), {7}... | custom-call | tf_op jit(solution)/shard_map/pallas_call | solution.py:250
  143.6 1.6 collective-permute-start.16
  149.6 11.5 %shard_map.70 = (f32[512,512]{1,0:T(8,128)S(1)}, f32[8,512]{1,0:T(8,128)S(1)}, f32[1312,128]{1,0:T(8,128)S(1)}, f32[1312,128]{1,0:T(8,128)}, f32[512,512]{1,0:T(...) custom-call(s32[2]{0:T(128)S(1)} %add_convert_fusion.4.flag_ref, ...), custom_call_target="tpu_custom_call", output_to_operand_aliasing={{0}: (1, {}), {1}: (6, {}), {5}: (7, {}), {6}: (8, {}), {7}... | custom-call | tf_op jit(solution)/shard_map/pallas_call | solution.py:250
  161.8 20.8 %shard_map.71.gains_ref = f32[8,512]{1,0:T(8,128)S(1)} custom-call(f32[512,512]{1,0:T(8,128)S(1)} %get-tuple-element.91.diag_ref, f32[1312,128]{1,0:T(8,128)S(1)} %collective-permute-done.17.rise_ref, f32[8,512]{1,0:T(8,128)S(1)} %get-tuple-element.93.source_ref), custom_call_target="tpu_custom_call" | custom-call | tf_op jit(solution)/shard_map/pallas_call | solution.py:250
  192.4 215.3 %collective-permute-done.25.below_ref = f32[8,512]{1,0:T(8,128)S(1)} collective-permute-done((f32[8,512]{1,0:T(8,128)S(1)}, f32[8,512]{1,0:T(8,128)S(1)}, u32[]{:S(2)}, u32[]{:S(2)}) %collective-permute-start.25) | collective-permute-done | bytes 16416 | tf_op jit(solution)/shard_map/ppermute | solution.py:329
  407.6 3.2 collective-permute-done.26.above_ref
  410.8 2.1 shard_map.76
  412.9 1.9 collective-permute-start.27
  414.8 4.9 %collective-permute-done.27 = f32[8,512]{1,0:T(8,128)S(1)} collective-permute-done((f32[8,512]{1,0:T(8,128)S(1)}, f32[8,512]{1,0:T(8,128)S(1)}, u32[]{:S(2)}, u32[]{:S(2)}) %collective-permute-start.27) | collective-permute-done | bytes 16416 | tf_op jit(solution)/shard_map/ppermute | solution.py:329
  (99 shorter events, 42.9 us)
Async XLA Ops:
  37.7 12.3 %collective-permute-start = (f32[1312,128]{1,0:T(8,128)}, f32[1312,128]{1,0:T(8,128)}, u32[]{:S(2)}, u32[]{:S(2)}) collective-permute-start(f32[1312,128]{1,0:T(8,128)} %get-tuple-element.54.rise_ref), channel_id=1, source_target_pairs={{1,0},{2,1},{3,2},{4,3},{5,4},{6,5},{7,6},{8,7},{9,8},{10,9},{11,1... | collective-permute-start | bytes 2015240 | tf_op jit(solution)/shard_map/ppermute | solution.py:329
  88.0 15.9 %collective-permute-start.3 = (f32[512,512]{1,0:T(8,128)}, f32[512,512]{1,0:T(8,128)}, u32[]{:S(2)}, u32[]{:S(2)}) collective-permute-start(f32[512,512]{1,0:T(8,128)} %get-tuple-element.62), channel_id=1, source_target_pairs={{0,1},{4,5},{8,9},{12,13},{16,17},{20,21},{24,25},{28,29}} | collective-permute-start | bytes 3145736 | tf_op jit(solution)/shard_map/ppermute | solution.py:329
  90.2 13.6 %collective-permute-start.4 = (f32[512,512]{1,0:T(8,128)}, f32[512,512]{1,0:T(8,128)}, u32[]{:S(2)}, u32[]{:S(2)}) collective-permute-start(f32[512,512]{1,0:T(8,128)} %get-tuple-element.62), channel_id=1, source_target_pairs={{2,1},{6,5},{10,9},{14,13},{18,17},{22,21},{26,25},{30,29}} | collective-permute-start | bytes 3145736 | tf_op jit(solution)/shard_map/ppermute | solution.py:329
  91.9 4.4 %collective-permute-start.1 = (f32[1312,128]{1,0:T(8,128)}, f32[1312,128]{1,0:T(8,128)}, u32[]{:S(2)}, u32[]{:S(2)}) collective-permute-start(f32[1312,128]{1,0:T(8,128)} %get-tuple-element.60), channel_id=1, source_target_pairs={{0,1},{2,3},{4,5},{6,7},{8,9},{10,11},{12,13},{14,15},{16,17},{18,... | collective-permute-start | bytes 2015240 | tf_op jit(solution)/shard_map/ppermute | solution.py:329
  94.0 9.9 %collective-permute-start.2 = (f32[1312,128]{1,0:T(8,128)}, f32[1312,128]{1,0:T(8,128)}, u32[]{:S(2)}, u32[]{:S(2)}) collective-permute-start(f32[1312,128]{1,0:T(8,128)} %get-tuple-element.61), channel_id=1, source_target_pairs={{2,1},{4,3},{6,5},{8,7},{10,9},{12,11},{14,13},{16,15},{18,17},{20... | collective-permute-start | bytes 2015240 | tf_op jit(solution)/shard_map/ppermute | solution.py:329
  112.4 6.4 %collective-permute-start.7 = (f32[512,512]{1,0:T(8,128)}, f32[512,512]{1,0:T(8,128)}, u32[]{:S(2)}, u32[]{:S(2)}) collective-permute-start(f32[512,512]{1,0:T(8,128)} %get-tuple-element.70), channel_id=1, source_target_pairs={{1,3},{9,11},{17,19},{25,27}} | collective-permute-start | bytes 3145736 | tf_op jit(solution)/shard_map/ppermute | solution.py:329
  114.0 4.8 %collective-permute-start.8 = (f32[512,512]{1,0:T(8,128)}, f32[512,512]{1,0:T(8,128)}, u32[]{:S(2)}, u32[]{:S(2)}) collective-permute-start(f32[512,512]{1,0:T(8,128)} %get-tuple-element.70), channel_id=1, source_target_pairs={{5,3},{13,11},{21,19},{29,27}} | collective-permute-start | bytes 3145736 | tf_op jit(solution)/shard_map/ppermute | solution.py:329
  115.6 3.1 collective-permute-start.5
  117.1 1.6 collective-permute-start.6
  127.0 6.4 %collective-permute-start.11 = (f32[512,512]{1,0:T(8,128)}, f32[512,512]{1,0:T(8,128)}, u32[]{:S(2)}, u32[]{:S(2)}) collective-permute-start(f32[512,512]{1,0:T(8,128)} %get-tuple-element.78), channel_id=1, source_target_pairs={{3,7},{19,23}} | collective-permute-start | bytes 3145736 | tf_op jit(solution)/shard_map/ppermute | solution.py:329
  128.7 4.8 %collective-permute-start.12 = (f32[512,512]{1,0:T(8,128)}, f32[512,512]{1,0:T(8,128)}, u32[]{:S(2)}, u32[]{:S(2)}) collective-permute-start(f32[512,512]{1,0:T(8,128)} %get-tuple-element.78), channel_id=1, source_target_pairs={{11,7},{27,23}} | collective-permute-start | bytes 3145736 | tf_op jit(solution)/shard_map/ppermute | solution.py:329
  130.3 3.1 collective-permute-start.10
  131.9 1.6 collective-permute-start.9
  142.0 6.4 %collective-permute-start.15 = (f32[512,512]{1,0:T(8,128)}, f32[512,512]{1,0:T(8,128)}, u32[]{:S(2)}, u32[]{:S(2)}) collective-permute-start(f32[512,512]{1,0:T(8,128)} %get-tuple-element.86), channel_id=1, source_target_pairs={{7,15}} | collective-permute-start | bytes 3145736 | tf_op jit(solution)/shard_map/ppermute | solution.py:329
  143.6 4.8 %collective-permute-start.16 = (f32[512,512]{1,0:T(8,128)}, f32[512,512]{1,0:T(8,128)}, u32[]{:S(2)}, u32[]{:S(2)}) collective-permute-start(f32[512,512]{1,0:T(8,128)} %get-tuple-element.86), channel_id=1, source_target_pairs={{23,15}} | collective-permute-start | bytes 3145736 | tf_op jit(solution)/shard_map/ppermute | solution.py:329
  145.2 3.1 collective-permute-start.13
  146.7 1.6 collective-permute-start.14
  161.1 0.7 collective-permute-start.17
  183.9 1.3 collective-permute-start.19
  185.8 1.3 collective-permute-start.21
  187.7 1.3 collective-permute-start.23
  189.6 218.0 %collective-permute-start.25 = (f32[8,512]{1,0:T(8,128)S(1)}, f32[8,512]{1,0:T(8,128)S(1)}, u32[]{:S(2)}, u32[]{:S(2)}) collective-permute-start(f32[8,512]{1,0:T(8,128)S(1)} %shard_map.75.gains_ref), channel_id=1, source_target_pairs={{1,2},{3,4},{5,6},{7,8},{9,10},{11,12},{13,14},{15,16},{17,18},{19... | collective-permute-start | bytes 49160 | tf_op jit(solution)/shard_map/ppermute | solution.py:329
  191.1 219.8 %collective-permute-start.26 = (f32[8,512]{1,0:T(8,128)S(1)}, f32[8,512]{1,0:T(8,128)S(1)}, u32[]{:S(2)}, u32[]{:S(2)}) collective-permute-start(f32[8,512]{1,0:T(8,128)S(1)} %shard_map.75.gains_ref), channel_id=1, source_target_pairs={{1,0},{3,2},{5,4},{7,6},{9,8},{11,10},{13,12},{15,14},{17,16},{19,... | collective-permute-start | bytes 49160 | tf_op jit(solution)/shard_map/ppermute | solution.py:329
  412.9 6.9 %collective-permute-start.27 = (f32[8,512]{1,0:T(8,128)S(1)}, f32[8,512]{1,0:T(8,128)S(1)}, u32[]{:S(2)}, u32[]{:S(2)}) collective-permute-start(f32[8,512]{1,0:T(8,128)S(1)} %shard_map.76), channel_id=1, source_target_pairs={{0,1},{1,2},{2,3},{3,4},{4,5},{5,6},{6,7},{7,8},{8,9},{9,10},{10,1... | collective-permute-start | bytes 49160 | tf_op jit(solution)/shard_map/ppermute | solution.py:329
  (19 other events, 247.5 us)

commit v4 on v3

--- a/solution.py
+++ b/solution.py
@@ -179,7 +179,7 @@
     else:
         above_ref, source_ref, _, _, _, *outs = refs
     diag_out, source_out, up_out, down_out, cross_out, c_ref, line_ref, x_ref, *holds = outs
-    below_hold, above_hold, up_ref, down_ref, cross_ref, sems = holds
+    hold_ref, packed_ref, cross_ref, sems = holds
     width = diag_ref.shape[0]
     for r, c, at in pairs(width):
         diag_out[cut(r), cut(c)] = (
@@ -189,11 +189,11 @@
 
     @pl.when(flag_ref[0] == 1)
     def _():
-        loads = [pltpu.make_async_copy(below_ref, below_hold, sems.at[0])]
+        loads = [pltpu.make_async_copy(below_ref, hold_ref.at[0], sems.at[0])]
         if first:
-            fill_square(above_hold, fall_ref)
+            fill_square(hold_ref.at[1], fall_ref)
         else:
-            loads.append(pltpu.make_async_copy(above_ref, above_hold, sems.at[1]))
+            loads.append(pltpu.make_async_copy(above_ref, hold_ref.at[1], sems.at[1]))
         for load in loads:
             load.start()
         x_ref[...] = diag_out[...]
@@ -201,26 +201,34 @@
         for load in loads:
             load.wait()
         half = width // 2
-        for side, ref in enumerate((below_hold, above_hold)):
-            c_ref[side, :, :half] = mm(ref[:, :half], x_ref[:half, :half], NT)
-            c_ref[side, :, half:] = mm(ref[...], x_ref[half:, :], NT)
+
+        @pl.loop(0, 2)
+        def _(side):
+            c_ref[side, :, :half] = mm(hold_ref[side, :, :half], x_ref[:half, :half], NT)
+            c_ref[side, :, half:] = mm(hold_ref[side], x_ref[half:, :], NT)
+
         line = mm(source_out[...], x_ref[...], NT)
         line_ref[...] = line
         cross_ref[...] = mm(c_ref[flag_ref[1]], c_ref[1 - flag_ref[1]], NT)
         stores = [
             pltpu.make_async_copy(ref, out, sems.at[2 + i])
             for i, (ref, out) in enumerate(
-                ((cross_ref, cross_out), (down_ref, down_out), (up_ref, up_out))
+                ((cross_ref, cross_out), (packed_ref.at[0], down_out), (packed_ref.at[1], up_out))
             )
         ]
         stores[0].start()
-        for side, ref in enumerate((down_ref, up_ref)):
+
+        @pl.loop(0, 2)
+        def _(side):
+            ref = packed_ref.at[side]
             put_line(ref, mm(line, c_ref[side], NT))
             for r in range(width // PANEL):
                 value = mm(c_ref[side, cut(r), :], c_ref[side, : (r + 1) * PANEL, :], NT)
                 for c in range(r + 1):
                     ref[cut(r * (r + 1) // 2 + c), :] = value[:, cut(c)]
-            stores[1 + side].start()
+
+        for store in stores[1:]:
+            store.start()
         for store in stores:
             store.wait()
 
@@ -272,7 +280,8 @@
 
     station = lax.broadcasted_iota(jnp.int32, (stations, rows), 0)
     touched = (station == one_ref[...]) | (station == two_ref[...])
-    keep = keep_ref[0].astype(jnp.float32)
+    own = pl.ds(pl.program_id(0), 1)
+    keep = keep_ref[own, :].astype(jnp.float32)
     vis = vis_ref[0].astype(jnp.float32)
     kept = touched & (keep > 0.0)
     plain = jnp.concatenate(
@@ -284,7 +293,7 @@
     normal_ref[0] += lax.dot_general(
         weighted, plain, (NT, ((), ())), preferred_element_type=jnp.float32
     )
-    data = obs_ref[0]
+    data = obs_ref[own, :]
     high = data.astype(jnp.bfloat16).astype(jnp.float32)
     middle = (data - high).astype(jnp.bfloat16).astype(jnp.float32)
     low = data - high - middle
@@ -306,8 +315,8 @@
         ],
         in_specs=[
             pl.BlockSpec((1, directions, chunk), lambda f, r: (f, 0, r)),
-            pl.BlockSpec((1, 1, chunk), lambda f, r: (f, 0, r)),
-            pl.BlockSpec((1, 1, chunk), lambda f, r: (f, 0, r)),
+            pl.BlockSpec((channels, chunk), lambda f, r: (0, r)),
+            pl.BlockSpec((channels, chunk), lambda f, r: (0, r)),
             pl.BlockSpec((1, chunk), lambda f, r: (0, r)),
             pl.BlockSpec((1, chunk), lambda f, r: (0, r)),
         ],
@@ -318,8 +327,8 @@
         compiler_params=pltpu.CompilerParams(vmem_limit_bytes=48 << 20),
     )(
         model_vis,
-        observed.reshape(channels, 1, rows),
-        row_keep.reshape(channels, 1, rows),
+        observed,
+        row_keep,
         station_one.reshape(1, rows),
         station_two.reshape(1, rows),
     )
@@ -380,7 +389,7 @@
             functools.partial(level_kernel, level == 0),
             (square, line, packed, packed, square, (2,) + square, line, square),
             flag, diag, rise, fall, *sides, source, c, solved, inverse,
-            scratch=(square, square, packed, packed, square),
+            scratch=((2,) + square, (2,) + packed, square),
             far_in=range(4, 4 + len(sides)),
             far_out=(2, 3, 4),
             sems=(pltpu.SemaphoreType.DMA((5,)),),

time: 429 us -> 429 us (level)
  Pallas kernels: 120 us -> 97.5 us
  waiting for transfers between devices: 239 us -> 259 us
  starting transfers between devices: 40.8 us -> 45.2 us
    pallas_call x12, Pallas kernels: 112 us -> 89.6 us  [call(): pl.pallas_call(kernel, out_shape=[jax.ShapeDtypeStruct(o, jnp.float32) fo...]
    ppermute x28, waiting for transfers between devices: 239 us -> 259 us  [move(): return lax.ppermute(block, 'freq', route)]
    ppermute x28, starting transfers between devices: 40.8 us -> 45.2 us  [move(): return lax.ppermute(block, 'freq', route)]
    unnamed x30 -> x34, local copies, waits for them, and re-layouts: 14.6 us -> 16.2 us
where the time goes in v4:
time: 429 us; the launch traced here: 422 us
  waiting for transfers between devices  259 us (60%)
  Pallas kernels  97.5 us (23%)
  starting transfers between devices  45.2 us (11%)
  local copies, waits for them, and re-layouts  17.9 us (4%)
    ppermute x28, waiting for transfers between devices, move(): return lax.ppermute(block, 'freq', route)  259 us
    pallas_call x12, Pallas kernels, call(): pl.pallas_call(kernel, out_shape=[jax.ShapeDtypeStruct(o, jnp.float32) fo...  89.6 us
    ppermute x28, starting transfers between devices, move(): return lax.ppermute(block, 'freq', route)  45.2 us
    unnamed x34, local copies, waits for them, and re-layouts  16.2 us
  transfers between devices with their start and end apart: 28, of which 5 were waited for; matrix products, arithmetic and copies ran while one was open for 0% of the time, Pallas kernels for 0%

profile of v4, /device:TPU:8, one launch (start us, length us, event | category | flops | bytes accessed | tf_op | source)
XLA Modules:
  0.0 422.2 jit_solution(11456871800627107981)
XLA Ops:
  4.8 7.9 %shard_map.64 = (f32[2,512,512]{2,1,0:T(8,128)S(1)}, f32[2,8,512]{2,1,0:T(8,128)S(1)}) custom-call(bf16[2,8,4096]{2,1,0:T(8,128)(2,1)S(1)} %copy-done.12, f32[2,4096]{1,0:T(2,128)S(1)} %copy-done.13, s32[2,4096]{1,0:T(2,128)S(1)} %copy-done.14, s32[1,4096]{1,0:T(1,128)S(1)} %bitcast.18, s32[1,4096]{1,0:T(1,128)S(1)} %bitcast.19), custom_call_target="tpu_custom_call" | custom-call | tf_op jit(solution)/shard_map/pallas_call | solution.py:309
  14.1 22.6 %shard_map.65 = (f32[512,512]{1,0:T(8,128)S(1)}, f32[1312,128]{1,0:T(8,128)}, f32[8,512]{1,0:T(8,128)S(1)}, f32[2,512,512]{2,1,0:T(8,128)S(1)}, f32[8,512]{1,0:T(8,128)S(1)}, /*index=5*/f32[512,512]{1,0:T(8,128)S(1)}) custom-call(f32[512,512]{1,0:T(8,128)S(1)} %get-tuple-element.97.diag_ref, f32[8,512]{1,0:T(8,128)S(1)} %pad.12.source_ref, ...), custom_call_target="tpu_custom_call" | custom-call | tf_op jit(solution)/shard_map/pallas_call | solution.py:258
  37.7 3.6 collective-permute-start
  41.4 8.5 %collective-permute-done.fall_ref = f32[1312,128]{1,0:T(8,128)} collective-permute-done((f32[1312,128]{1,0:T(8,128)}, f32[1312,128]{1,0:T(8,128)}, u32[]{:S(2)}, u32[]{:S(2)}) %collective-permute-start) | collective-permute-done | bytes 671776 | tf_op jit(solution)/shard_map/ppermute | solution.py:338
  52.3 35.2 %shard_map.66 = (f32[512,512]{1,0:T(8,128)S(1)}, f32[8,512]{1,0:T(8,128)S(1)}, f32[1312,128]{1,0:T(8,128)}, f32[1312,128]{1,0:T(8,128)}, f32[512,512]{1,0:T(8,12...) custom-call(s32[2]{0:T(128)S(1)} %add_convert_fusion.flag_ref, ...), custom_call_target="tpu_custom_call", output_to_operand_aliasing={{0}: (1, {}), {1}: (5, {}), {5}: (6, {}), {6}: (7, {}), {7}... | custom-call | tf_op jit(solution)/shard_map/pallas_call | solution.py:258
  88.5 2.3 collective-permute-start.3
  92.4 2.1 collective-permute-start.1
  94.5 2.3 collective-permute-start.2
  97.0 7.4 %collective-permute-done.2.fall_ref = f32[1312,128]{1,0:T(8,128)} collective-permute-done((f32[1312,128]{1,0:T(8,128)}, f32[1312,128]{1,0:T(8,128)}, u32[]{:S(2)}, u32[]{:S(2)}) %collective-permute-start.2) | collective-permute-done | bytes 671776 | tf_op jit(solution)/shard_map/ppermute | solution.py:338
  105.6 1.7 shard_map.67
  113.1 1.8 collective-permute-start.6
  116.2 1.7 shard_map.68
  118.9 1.6 collective-permute-start.11
  123.7 1.9 collective-permute-start.9
  126.9 1.7 shard_map.69
  132.9 1.7 collective-permute-start.13
  137.4 1.7 shard_map.70
  139.1 4.2 collective-permute-start.17
  143.3 20.8 %shard_map.71.gains_ref = f32[8,512]{1,0:T(8,128)S(1)} custom-call(f32[512,512]{1,0:T(8,128)S(1)} %get-tuple-element.91.diag_ref, f32[1312,128]{1,0:T(8,128)S(1)} %collective-permute-done.17.rise_ref, f32[8,512]{1,0:T(8,128)S(1)} %get-tuple-element.93.source_ref), custom_call_target="tpu_custom_call" | custom-call | tf_op jit(solution)/shard_map/pallas_call | solution.py:258
  173.9 234.5 %collective-permute-done.25.below_ref = f32[8,512]{1,0:T(8,128)S(1)} collective-permute-done((f32[8,512]{1,0:T(8,128)S(1)}, f32[8,512]{1,0:T(8,128)S(1)}, u32[]{:S(2)}, u32[]{:S(2)}) %collective-permute-start.25) | collective-permute-done | bytes 16416 | tf_op jit(solution)/shard_map/ppermute | solution.py:338
  408.4 3.2 collective-permute-done.26.above_ref
  411.6 2.1 shard_map.76
  413.7 1.9 collective-permute-start.27
  415.7 4.9 %collective-permute-done.27 = f32[8,512]{1,0:T(8,128)S(1)} collective-permute-done((f32[8,512]{1,0:T(8,128)S(1)}, f32[8,512]{1,0:T(8,128)S(1)}, u32[]{:S(2)}, u32[]{:S(2)}) %collective-permute-start.27) | collective-permute-done | bytes 16416 | tf_op jit(solution)/shard_map/ppermute | solution.py:338
  (101 shorter events, 44.2 us)
Async XLA Ops:
  37.7 12.2 %collective-permute-start = (f32[1312,128]{1,0:T(8,128)}, f32[1312,128]{1,0:T(8,128)}, u32[]{:S(2)}, u32[]{:S(2)}) collective-permute-start(f32[1312,128]{1,0:T(8,128)} %get-tuple-element.54.rise_ref), channel_id=1, source_target_pairs={{1,0},{2,1},{3,2},{4,3},{5,4},{6,5},{7,6},{8,7},{9,8},{10,9},{11,1... | collective-permute-start | bytes 2015240 | tf_op jit(solution)/shard_map/ppermute | solution.py:338
  88.5 15.9 %collective-permute-start.3 = (f32[512,512]{1,0:T(8,128)}, f32[512,512]{1,0:T(8,128)}, u32[]{:S(2)}, u32[]{:S(2)}) collective-permute-start(f32[512,512]{1,0:T(8,128)} %get-tuple-element.62), channel_id=1, source_target_pairs={{0,1},{4,5},{8,9},{12,13},{16,17},{20,21},{24,25},{28,29}} | collective-permute-start | bytes 3145736 | tf_op jit(solution)/shard_map/ppermute | solution.py:338
  90.8 13.6 %collective-permute-start.4 = (f32[512,512]{1,0:T(8,128)}, f32[512,512]{1,0:T(8,128)}, u32[]{:S(2)}, u32[]{:S(2)}) collective-permute-start(f32[512,512]{1,0:T(8,128)} %get-tuple-element.62), channel_id=1, source_target_pairs={{2,1},{6,5},{10,9},{14,13},{18,17},{22,21},{26,25},{30,29}} | collective-permute-start | bytes 3145736 | tf_op jit(solution)/shard_map/ppermute | solution.py:338
  92.4 4.6 %collective-permute-start.1 = (f32[1312,128]{1,0:T(8,128)}, f32[1312,128]{1,0:T(8,128)}, u32[]{:S(2)}, u32[]{:S(2)}) collective-permute-start(f32[1312,128]{1,0:T(8,128)} %get-tuple-element.60), channel_id=1, source_target_pairs={{0,1},{2,3},{4,5},{6,7},{8,9},{10,11},{12,13},{14,15},{16,17},{18,... | collective-permute-start | bytes 2015240 | tf_op jit(solution)/shard_map/ppermute | solution.py:338
  94.5 9.9 %collective-permute-start.2 = (f32[1312,128]{1,0:T(8,128)}, f32[1312,128]{1,0:T(8,128)}, u32[]{:S(2)}, u32[]{:S(2)}) collective-permute-start(f32[1312,128]{1,0:T(8,128)} %get-tuple-element.61), channel_id=1, source_target_pairs={{2,1},{4,3},{6,5},{8,7},{10,9},{12,11},{14,13},{16,15},{18,17},{20... | collective-permute-start | bytes 2015240 | tf_op jit(solution)/shard_map/ppermute | solution.py:338
  108.3 6.6 %collective-permute-start.7 = (f32[512,512]{1,0:T(8,128)}, f32[512,512]{1,0:T(8,128)}, u32[]{:S(2)}, u32[]{:S(2)}) collective-permute-start(f32[512,512]{1,0:T(8,128)} %get-tuple-element.70), channel_id=1, source_target_pairs={{1,3},{9,11},{17,19},{25,27}} | collective-permute-start | bytes 3145736 | tf_op jit(solution)/shard_map/ppermute | solution.py:338
  110.0 5.0 %collective-permute-start.8 = (f32[512,512]{1,0:T(8,128)}, f32[512,512]{1,0:T(8,128)}, u32[]{:S(2)}, u32[]{:S(2)}) collective-permute-start(f32[512,512]{1,0:T(8,128)} %get-tuple-element.70), channel_id=1, source_target_pairs={{5,3},{13,11},{21,19},{29,27}} | collective-permute-start | bytes 3145736 | tf_op jit(solution)/shard_map/ppermute | solution.py:338
  111.6 3.3 collective-permute-start.5
  113.1 1.9 collective-permute-start.6
  118.9 6.8 %collective-permute-start.11 = (f32[512,512]{1,0:T(8,128)}, f32[512,512]{1,0:T(8,128)}, u32[]{:S(2)}, u32[]{:S(2)}) collective-permute-start(f32[512,512]{1,0:T(8,128)} %get-tuple-element.78), channel_id=1, source_target_pairs={{3,7},{19,23}} | collective-permute-start | bytes 3145736 | tf_op jit(solution)/shard_map/ppermute | solution.py:338
  120.5 5.2 %collective-permute-start.12 = (f32[512,512]{1,0:T(8,128)}, f32[512,512]{1,0:T(8,128)}, u32[]{:S(2)}, u32[]{:S(2)}) collective-permute-start(f32[512,512]{1,0:T(8,128)} %get-tuple-element.78), channel_id=1, source_target_pairs={{11,7},{27,23}} | collective-permute-start | bytes 3145736 | tf_op jit(solution)/shard_map/ppermute | solution.py:338
  122.1 3.5 collective-permute-start.10
  123.7 2.0 collective-permute-start.9
  129.6 6.6 %collective-permute-start.15 = (f32[512,512]{1,0:T(8,128)}, f32[512,512]{1,0:T(8,128)}, u32[]{:S(2)}, u32[]{:S(2)}) collective-permute-start(f32[512,512]{1,0:T(8,128)} %get-tuple-element.86), channel_id=1, source_target_pairs={{7,15}} | collective-permute-start | bytes 3145736 | tf_op jit(solution)/shard_map/ppermute | solution.py:338
  131.2 4.9 %collective-permute-start.16 = (f32[512,512]{1,0:T(8,128)}, f32[512,512]{1,0:T(8,128)}, u32[]{:S(2)}, u32[]{:S(2)}) collective-permute-start(f32[512,512]{1,0:T(8,128)} %get-tuple-element.86), channel_id=1, source_target_pairs={{23,15}} | collective-permute-start | bytes 3145736 | tf_op jit(solution)/shard_map/ppermute | solution.py:338
  132.9 3.3 collective-permute-start.13
  134.6 1.6 collective-permute-start.14
  139.1 4.2 collective-permute-start.17
  165.4 1.3 collective-permute-start.19
  167.3 1.3 collective-permute-start.21
  169.2 1.3 collective-permute-start.23
  171.2 237.3 %collective-permute-start.25 = (f32[8,512]{1,0:T(8,128)S(1)}, f32[8,512]{1,0:T(8,128)S(1)}, u32[]{:S(2)}, u32[]{:S(2)}) collective-permute-start(f32[8,512]{1,0:T(8,128)S(1)} %shard_map.75.gains_ref), channel_id=1, source_target_pairs={{1,2},{3,4},{5,6},{7,8},{9,10},{11,12},{13,14},{15,16},{17,18},{19... | collective-permute-start | bytes 49160 | tf_op jit(solution)/shard_map/ppermute | solution.py:338
  172.6 239.0 %collective-permute-start.26 = (f32[8,512]{1,0:T(8,128)S(1)}, f32[8,512]{1,0:T(8,128)S(1)}, u32[]{:S(2)}, u32[]{:S(2)}) collective-permute-start(f32[8,512]{1,0:T(8,128)S(1)} %shard_map.75.gains_ref), channel_id=1, source_target_pairs={{1,0},{3,2},{5,4},{7,6},{9,8},{11,10},{13,12},{15,14},{17,16},{19,... | collective-permute-start | bytes 49160 | tf_op jit(solution)/shard_map/ppermute | solution.py:338
  413.7 6.9 %collective-permute-start.27 = (f32[8,512]{1,0:T(8,128)S(1)}, f32[8,512]{1,0:T(8,128)S(1)}, u32[]{:S(2)}, u32[]{:S(2)}) collective-permute-start(f32[8,512]{1,0:T(8,128)S(1)} %shard_map.76), channel_id=1, source_target_pairs={{0,1},{1,2},{2,3},{3,4},{4,5},{5,6},{6,7},{7,8},{8,9},{9,10},{10,1... | collective-permute-start | bytes 49160 | tf_op jit(solution)/shard_map/ppermute | solution.py:338
  (21 other events, 268.4 us)
